TPU v7x, 128 devices: a whole 4x4x4 slice. The times are simulated.
128 devices in a mesh: dp: 8 (over z, y_hi), fsdp: 16 (over y_lo, x, core).
Axes of the slice: x: 4, y: 4 (y_hi: 2, y_lo: 2; y = y_hi * 2 + y_lo), z: 4, core: 2. Of those that a mesh axis runs over, the one named last changes fastest.
Arguments:
- tokens: bfloat16 [16, 1024, 2048], P('dp', 'fsdp'), may hold values from -6 to 6
- w_qkv: bfloat16 [2048, 3072], P('fsdp', 'dp'), may hold values from -0.1875 to 0.1875
- w_out: bfloat16 [1024, 2048], P('fsdp', 'dp'), may hold values from -0.375 to 0.375
- ln_gain: float32 [2048], replicated, may hold values from 0.5 to 1.5
- ln_bias: float32 [2048], replicated, may hold values from -3 to 3
- kv_pool: bfloat16 [64, 128, 2048], P('fsdp'), may hold values from -300 to 300
- page_table: int32 [4, 16], replicated, may hold values from 0 to 63, as said below
- prefix_len: int32 [4], replicated, may hold values from 1 to 2048, as said below
- group_of: int32 [16], P('dp'), may hold values from 0 to 3, as said below
Outputs:
- hidden_out: bfloat16 [16, 1024, 2048], P('dp', 'fsdp')
- new_cache: bfloat16 [16, 1024, 2048], P('dp', 'fsdp')
Inputs may be any that keep to these rules, and one draw needn't show every extreme that they name: `page_table`: a permutation of the pool's slots. `prefix_len`: some group's prefix is exactly 2048 long. `group_of`: each group has 4 requests.
All inputs are finite; a program needn't handle non-finite values.
Results may differ from a plain program's by a relative error of at most 0.012.
The roundings to bfloat16 on the way count: a program that leaves them out, or rounds other values in their place, can miss the bound.
Values may be sent and summed in bfloat16 or wider, within the bound.
A program may use at most 128 MiB of HBM per device.

v0:
```python
import math

import jax
import jax.numpy as jnp
from jax import lax
from jax.sharding import PartitionSpec as P

HD = 128


neg_big = -1e30
ln_eps = 1e-06


def attend_rows(
    queries, row_req, row_pos, row_group, row_len, key_rows, value_rows, key_req, key_pos, key_group
):
    row_count = queries.shape[0]
    heads = queries.shape[1]
    head_dim = queries.shape[2]
    block_rows = min(512, row_count)
    inv_root = 1.0 / math.sqrt(head_dim)

    def one_block(first_row):
        q_block = lax.dynamic_slice_in_dim(queries, first_row, block_rows, 0)
        req_block = lax.dynamic_slice_in_dim(row_req, first_row, block_rows, 0)
        pos_block = lax.dynamic_slice_in_dim(row_pos, first_row, block_rows, 0)
        group_block = lax.dynamic_slice_in_dim(row_group, first_row, block_rows, 0)
        len_block = lax.dynamic_slice_in_dim(row_len, first_row, block_rows, 0)
        scores = (
            jnp.einsum("nhd,khd->nhk", q_block, key_rows, preferred_element_type=jnp.float32)
            * inv_root
        )
        from_prefix = (key_group[None, :] == group_block[:, None]) & (
            key_pos[None, :] < len_block[:, None]
        )
        from_new = (key_req[None, :] == req_block[:, None]) & (
            key_pos[None, :] <= pos_block[:, None]
        )
        is_live = jnp.where(key_req[None, :] < 0, from_prefix, from_new)
        scores = jnp.where(is_live[:, None, :], scores, neg_big)
        row_max = jnp.max(scores, axis=2)
        expo = jnp.where(is_live[:, None, :], jnp.exp(scores - row_max[:, :, None]), 0.0)
        row_total = jnp.sum(expo, axis=2)
        summed = jnp.einsum(
            "nhk,khd->nhd",
            expo.astype(jnp.bfloat16),
            value_rows,
            preferred_element_type=jnp.float32,
        )
        return (summed, row_max, row_total)

    starts = jnp.arange(row_count // block_rows, dtype=jnp.int32) * block_rows
    summed, row_max, row_total = lax.map(one_block, starts)
    return (
        summed.reshape(row_count, heads, head_dim),
        row_max.reshape(row_count, heads),
        row_total.reshape(row_count, heads),
    )


def body(tokens, w_qkv, w_out, ln_gain, ln_bias, kv_pool, page_table, prefix_len, group_of):
    req_count = tokens.shape[0]
    tok_count = tokens.shape[1]
    width = tokens.shape[2]
    owners = lax.axis_size("fsdp")
    owner_index = lax.axis_index("fsdp")
    inner = w_out.shape[0] * owners
    heads = inner // HD
    new_len = tok_count * owners
    flat_rows = tokens.reshape(req_count * tok_count, width)
    qkv_cols, out_cols = (
        lax.all_gather(w_qkv, "dp", axis=1, tiled=True),
        lax.all_gather(w_out, "dp", axis=1, tiled=True),
    )
    left_rows = flat_rows
    qkv_sum = jnp.dot(
        left_rows,
        lax.all_gather(qkv_cols, "fsdp", axis=0, tiled=True),
        preferred_element_type=jnp.float32,
    )
    qkv = qkv_sum.astype(jnp.bfloat16).reshape(req_count, tok_count, 3 * inner)
    own_queries = qkv[:, :, :inner]
    new_cache = qkv[:, :, inner:]
    own_keys = qkv[:, :, inner : 2 * inner]
    own_values = qkv[:, :, 2 * inner :]
    slot_count = kv_pool.shape[0]
    page_len = kv_pool.shape[1]
    group_count = page_table.shape[0]
    page_slots = page_table.shape[1]
    slot_ids = owner_index * slot_count + jnp.arange(slot_count, dtype=jnp.int32)
    matches = (page_table[:, :, None] == slot_ids[None, None, :]).astype(jnp.int32)
    slot_group = jnp.sum(
        matches * jnp.arange(group_count, dtype=jnp.int32)[:, None, None], axis=(0, 1)
    )
    slot_page = jnp.sum(
        matches * jnp.arange(page_slots, dtype=jnp.int32)[None, :, None], axis=(0, 1)
    )
    pool_pos = (
        slot_page[:, None] * page_len + jnp.arange(page_len, dtype=jnp.int32)[None, :]
    ).reshape(-1)
    pool_group = jnp.broadcast_to(slot_group[:, None], (slot_count, page_len)).reshape(-1)
    pool_req = jnp.full(pool_pos.shape, -1, jnp.int32)
    pool_keys = kv_pool[:, :, :inner].reshape(slot_count * page_len, heads, HD)
    pool_values = kv_pool[:, :, inner:].reshape(slot_count * page_len, heads, HD)
    member = (group_of[:, None] == jnp.arange(group_count, dtype=jnp.int32)[None, :]).astype(
        jnp.int32
    )
    request_len = jnp.sum(member * prefix_len[None, :], axis=1)

    def describe(row_positions):
        span_len = row_positions.shape[0]
        req_ids = jnp.broadcast_to(
            jnp.arange(req_count, dtype=jnp.int32)[:, None], (req_count, span_len)
        ).reshape(-1)
        pos_ids = jnp.broadcast_to(row_positions[None, :], (req_count, span_len)).reshape(-1)
        group_ids = jnp.broadcast_to(group_of[:, None], (req_count, span_len)).reshape(-1)
        len_ids = jnp.broadcast_to(request_len[:, None], (req_count, span_len)).reshape(-1)
        return (req_ids, pos_ids, group_ids, len_ids)

    all_positions = jnp.arange(new_len, dtype=jnp.int32)
    own_positions = owner_index * tok_count + jnp.arange(tok_count, dtype=jnp.int32)
    all_info = describe(all_positions)
    own_info = describe(own_positions)
    whole_q, whole_k, whole_v = (
        lax.all_gather(own_queries, "fsdp", axis=1, tiled=True),
        lax.all_gather(own_keys, "fsdp", axis=1, tiled=True),
        lax.all_gather(own_values, "fsdp", axis=1, tiled=True),
    )
    owner_sum, owner_max, owner_total = attend_rows(
        whole_q.reshape(req_count * new_len, heads, HD),
        all_info[0],
        all_info[1],
        all_info[2],
        all_info[3],
        pool_keys,
        pool_values,
        pool_req,
        pool_pos,
        pool_group,
    )
    owner_norm = (owner_sum / jnp.maximum(owner_total, 1.0)[:, :, None]).astype(jnp.bfloat16)
    part_norm = owner_norm.reshape(1, req_count, new_len, inner)
    part_max = owner_max.reshape(1, req_count, new_len, heads)
    part_total = owner_total.reshape(1, req_count, new_len, heads)
    got_norm = lax.all_to_all(part_norm, "fsdp", split_axis=2, concat_axis=0, tiled=True)
    got_max, got_total = (
        lax.all_to_all(part_max, "fsdp", split_axis=2, concat_axis=0, tiled=True),
        lax.all_to_all(part_total, "fsdp", split_axis=2, concat_axis=0, tiled=True),
    )
    local_sum, local_max, local_total = attend_rows(
        own_queries.reshape(req_count * tok_count, heads, HD),
        own_info[0],
        own_info[1],
        own_info[2],
        own_info[3],
        whole_k.reshape(req_count * new_len, heads, HD),
        whole_v.reshape(req_count * new_len, heads, HD),
        all_info[0],
        all_info[1],
        jnp.full(all_info[0].shape, -1, jnp.int32),
    )
    local_sum = local_sum.reshape(req_count, tok_count, heads, HD)
    local_max = local_max.reshape(req_count, tok_count, heads)
    local_total = local_total.reshape(req_count, tok_count, heads)
    overall = jnp.maximum(jnp.max(got_max, axis=0), local_max)
    factor = got_total * jnp.exp(got_max - overall[None])
    local_factor = jnp.exp(local_max - overall)
    part_count = got_norm.shape[0]
    normed_parts = got_norm.reshape(part_count, req_count, tok_count, heads, HD)
    numer = jnp.sum(normed_parts.astype(jnp.float32) * factor[..., None], axis=0)
    numer = numer + local_sum * local_factor[..., None]
    denom = jnp.sum(factor, axis=0) + local_total * local_factor
    attn = (numer / denom[..., None]).reshape(req_count * tok_count, inner).astype(jnp.bfloat16)
    left_rows = attn
    proj = jnp.dot(
        left_rows,
        lax.all_gather(out_cols, "fsdp", axis=0, tiled=True),
        preferred_element_type=jnp.float32,
    )
    mixed = flat_rows.astype(jnp.float32) + proj
    mean_row = jnp.mean(mixed, axis=1, keepdims=True)
    centred = mixed - mean_row
    var_row = jnp.mean(centred * centred, axis=1, keepdims=True)
    normed = centred * lax.rsqrt(var_row + ln_eps) * ln_gain[None, :] + ln_bias[None, :]
    hidden_out = normed.astype(jnp.bfloat16).reshape(req_count, tok_count, width)
    return (hidden_out, new_cache)


def solution(mesh):
    in_specs = (
        P("dp", "fsdp", None),
        P("fsdp", "dp"),
        P("fsdp", "dp"),
        P(),
        P(),
        P("fsdp", None, None),
        P(),
        P(),
        P("dp"),
    )
    out_specs = (P("dp", "fsdp", None), P("dp", "fsdp", None))
    return jax.shard_map(body, mesh=mesh, in_specs=in_specs, out_specs=out_specs, check_vma=False)
```

profile of v0, /device:TPU:1, one launch (start us, length us, event | category | flops | bytes accessed | tf_op | source)
XLA Modules:
  0.0 372.0 jit_solution(6619067220473818297)
XLA Ops:
  7.2 36.4 %all_gather.21 = bf16[128,3072]{1,0:T(8,128)(2,1)} all-gather(bf16[128,384]{1,0:T(8,128)(2,1)} %param.12), channel_id=1, replica_groups=mesh['dp'=8,'fsdp'=16] {'dp'}, dimensions={1}, use_global_device_ids=true | all-gather | bytes 884736 | tf_op jit(solution)/shard_map/all_gather | solution.py:73
  43.6 78.5 %all-gather.6.cloned.1.call-done = bf16[2048,3072]{1,0:T(8,128)(2,1)} async-done(((bf16[128,3072]{1,0:T(8,128)(2,1)}), bf16[2048,3072]{1,0:T(8,128)(2,1)}) %all-gather.6.cloned.1.call-update) | async-done | bytes 12582928 | tf_op jit(solution)/shard_map/all_gather | solution.py:79
  122.2 6.6 %convolution_convert_fusion = bf16[128,3072]{1,0:T(8,128)(2,1)S(1)} fusion(bf16[128,2048]{1,0:T(8,128)(2,1)} %bitcast.180, bf16[2048,3072]{1,0:T(8,128)(2,1)} %all-gather.6.cloned.1.call-done), kind=kOutput, calls=%fused_computation.42 | convolution fusion | flops 1611005952 | bytes 13893632 | tf_op jit(solution)/shard_map/dot_general | solution.py:77
  131.1 32.2 %all_gather.26 = bf16[64,2048]{1,0:T(8,128)(2,1)} all-gather(bf16[64,256]{1,0:T(8,128)(2,1)S(1)} %copy-done.2), channel_id=1, replica_groups=mesh['dp'=8,'fsdp'=16] {'dp'}, dimensions={1}, use_global_device_ids=true | all-gather | bytes 294912 | tf_op jit(solution)/shard_map/all_gather | solution.py:74
  163.9 1.7 fusion.48
  167.0 1.6 all-gather.8.cloned.1.call-done
  168.7 5.2 %copy.131 = bf16[256,8,8,128]{3,2,1,0:T(8,128)(2,1)} copy(bf16[256,8,8,128]{3,1,2,0:T(8,128)(2,1)} %bitcast.169) | data formatting | bytes 8388608
  173.9 54.3 %while.4 = (s32[]{:T(128)}, f32[4,512,8,128]{3,2,1,0:T(8,128)}, f32[4,512,8]{1,2,0:T(8,128)S(1)}, f32[4,512,8]{1,2,0:T(8,128)S(1)}, s32[4]{0:T(128)S(1)}, /*inde...) while((s32[]{:T(128)}, f32[4,512,8,128]{3,2,1,0:T(8,128)}, ...), condition=%wide.region_6.7_spmd.clone, body=%wide.region_3.6_spmd.clone.sunk | while | flops 1101783552 | bytes 37900532 | solution.py:54
  178.2 1.6 bitcast_reduce_fusion.3
  179.8 3.0 fusion.65
  182.8 2.6 copy_dynamic-update-slice_fusion.2
  185.4 2.0 fusion.66
  190.5 1.3 constant_dynamic-slice_fusion.2
  191.8 1.6 bitcast_reduce_fusion.3
  193.5 3.0 fusion.65
  196.5 2.5 copy_dynamic-update-slice_fusion.2
  199.0 2.0 fusion.66
  205.4 1.6 bitcast_reduce_fusion.3
  207.0 3.0 fusion.65
  210.0 2.6 copy_dynamic-update-slice_fusion.2
  212.6 2.0 fusion.66
  219.0 1.6 bitcast_reduce_fusion.3
  220.6 3.0 fusion.65
  223.6 2.5 copy_dynamic-update-slice_fusion.2
  226.1 2.0 fusion.66
  228.7 2.2 reshape.384
  230.9 9.9 %all-to-all-start.2 = ((f32[16,1,1024]{2,1,0:T(1,128)}), f32[16,1,1024]{2,1,0:T(1,128)S(1)}, u32[]{:S(2)}, u32[]{:S(2)}) async-start(f32[16,1,1024]{2,1,0:T(1,128)} %reshape.384), calls=%async_computation.2 | async-start | bytes 131072 | tf_op jit(solution)/shard_map/all_to_all | solution.py:148
  241.4 2.2 reshape.386
  243.7 9.3 %reshape.377 = f32[1,2,1024,1024]{3,2,1,0:T(8,128)} reshape(f32[4,512,8,128]{3,2,1,0:T(8,128)} %get-tuple-element.136) | data formatting | bytes 16777216 | tf_op jit(solution)/shard_map/reshape | solution.py:56
  253.3 6.4 %div.34 = f32[2048,8,128]{2,1,0:T(8,128)} broadcast(f32[2048,8]{1,0:T(8,128)S(1)} %copy.100), dimensions={0,1} | broadcast | bytes 8454144 | tf_op jit(solution)/shard_map/div | solution.py:142
  259.6 9.3 %div.35 = f32[1,2,1024,1024]{3,2,1,0:T(8,128)} reshape(f32[2048,8,128]{2,1,0:T(8,128)} %div.34) | data formatting | bytes 16777216 | tf_op jit(solution)/shard_map/div | solution.py:142
  268.9 5.7 %all-to-all-start.1 = ((f32[16,1,1024]{2,1,0:T(1,128)}), f32[16,1,1024]{2,1,0:T(1,128)S(1)}, u32[]{:S(2)}, u32[]{:S(2)}) async-start(f32[16,1,1024]{2,1,0:T(1,128)} %reshape.386), calls=%async_computation.1 | async-start | bytes 131072 | tf_op jit(solution)/shard_map/all_to_all | solution.py:149
  274.7 7.8 %divide_convert_fusion = bf16[1,2,1024,1024]{3,2,1,0:T(8,128)(2,1)S(1)} fusion(f32[1,2,1024,1024]{3,2,1,0:T(8,128)} %reshape.377, f32[1,2,1024,1024]{3,2,1,0:T(8,128)} %div.35), kind=kLoop, calls=%fused_computation.30 | loop fusion | flops 4194304 | bytes 20971520 | tf_op jit(solution)/shard_map/convert_element_type | solution.py:142
  282.5 6.2 %copy.101 = bf16[1,2,1024,1024]{3,1,0,2:T(2,128)(2,1)} copy(bf16[1,2,1024,1024]{3,2,1,0:T(8,128)(2,1)S(1)} %divide_convert_fusion) | data formatting | bytes 8388608 | tf_op jit(solution)/shard_map/convert_element_type | solution.py:142
  288.8 6.0 %all-to-all-start = ((bf16[1,2,1024,1024]{3,1,0,2:T(2,128)(2,1)}), bf16[1,2,1024,1024]{3,1,0,2:T(2,128)(2,1)}, u32[]{:S(2)}, u32[]{:S(2)}) async-start(bf16[1,2,1024,1024]{3,1,0,2:T(2,128)(2,1)} %copy.101), calls=%async_computation | async-start | bytes 8388608 | tf_op jit(solution)/shard_map/all_to_all | solution.py:146
  294.8 1.7 and_select_fusion
  297.5 3.3 copy.136
  300.8 4.9 %fusion.22 = (f32[128,8]{0,1:T(8,128)S(1)}, f32[8,2048,128]{2,1,0:T(8,128)}) fusion(pred[128,2048]{0,1:T(8,128)(4,1)S(1)} %and_select_fusion, bf16[128,8,128]{2,1,0:T(8,128)(2,1)S(1)} %bitcast.189, bf16[2048,8,128]{2,1,0:T(8,128)(2,1)S(1)} %bitcast.170), kind=kOutput, calls=%fused_computation.31 | convolution fusion | flops 543161344 | bytes 13111296 | tf_op jit(solution)/shard_map/while/body/eval_jaxpr/nhd,khd->nhk/dot_general | solution.py:31
  305.7 4.5 %fusion.23 = f32[128,8]{0,1:T(8,128)S(1)} fusion(f32[8,2048,128]{2,1,0:T(8,128)} %get-tuple-element.280, f32[128,8]{0,1:T(8,128)S(1)} %get-tuple-element.279, pred[128,2048]{0,1:T(8,128)(4,1)S(1)} %and_select_fusion), kind=kLoop, calls=%fused_computation.32 | loop fusion | flops 10484736 | bytes 8658944 | tf_op jit(solution)/shard_map/while/body/eval_jaxpr/reduce_sum | solution.py:44
  310.3 3.3 copy.138
  313.6 5.7 %fusion.25 = f32[8,128,128]{2,1,0:T(8,128)S(1)} fusion(bf16[2048,8,128]{2,1,0:T(8,128)(2,1)S(1)} %bitcast.171, f32[8,2048,128]{2,1,0:T(8,128)} %get-tuple-element.280, f32[128,8]{0,1:T(8,128)S(1)} %get-tuple-element.279, pred[128,2048]{0,1:T(8,128)(4,1)S(1)} %and_select_fusion), kind=kOutput, calls=%fused_computation.34 | convolution fusion | flops 547356672 | bytes 13373440 | tf_op jit(solution)/shard_map/while/body/eval_jaxpr/nhk,khd->nhd/dot_general | solution.py:45
  320.8 1.6 reshape.385
  323.7 1.6 reshape.387
  326.7 4.6 %mul.121 = f32[16,2,64,8,128]{4,3,1,2,0:T(8,128)} broadcast(f32[16,2,64,8]{3,1,2,0:T(2,128)S(1)} %copy.109), dimensions={0,1,2,3} | broadcast | bytes 8454144 | tf_op jit(solution)/shard_map/mul | solution.py:171
  331.3 11.0 %mul.122 = f32[16,1,2,64,1024]{4,2,3,0,1:T(2,128)} reshape(f32[16,2,64,8,128]{4,3,1,2,0:T(8,128)} %mul.121) | data formatting | bytes 16777216 | tf_op jit(solution)/shard_map/mul | solution.py:171
  342.2 8.3 %all-to-all-done = bf16[1,2,1024,1024]{3,1,0,2:T(2,128)(2,1)} async-done(((bf16[1,2,1024,1024]{3,1,0,2:T(2,128)(2,1)}), bf16[1,2,1024,1024]{3,1,0,2:T(2,128)(2,1)}, u32[]{:S(2)}, u32[]{:S(2)}) %all-to-all-start) | async-done | bytes 4194336 | tf_op jit(solution)/shard_map/all_to_all | solution.py:146
  350.5 9.5 %fusion.21 = f32[2,64,1024]{2,0,1:T(2,128)S(1)} fusion(f32[16,1,2,64,1024]{4,2,3,0,1:T(2,128)} %mul.122, bf16[1,2,16,64,1024]{4,1,3,2,0:T(2,128)(2,1)} %bitcast.26), kind=kLoop, calls=%fused_computation.27 | loop fusion | flops 6160384 | bytes 13107200 | tf_op jit(solution)/shard_map/reduce_sum | solution.py:171
  360.9 3.0 fusion.50
  (120 shorter events, 21.6 us)
Async XLA Ops:
  7.2 115.0 %all-gather.6.cloned.1.call-start = ((), (), s32[]{:S(2)}) async-start(), calls=%async_computation.3 | async-start | bytes 13369344 | tf_op jit(solution)/shard_map/all_gather | solution.py:79
  43.6 125.1 %all-gather.8.cloned.1.call-start = ((), (), s32[]{:S(2)}) async-start(), calls=%async_computation.4 | async-start | bytes 4456448 | tf_op jit(solution)/shard_map/all_gather | solution.py:126
  122.2 8.9 %copy-start.2 = (bf16[64,256]{1,0:T(8,128)(2,1)S(1)}, bf16[64,256]{1,0:T(8,128)(2,1)}, u32[]{:S(2)}) copy-start(bf16[64,256]{1,0:T(8,128)(2,1)} %param.13) | copy-start | bytes 98308
  122.2 41.2 %copy-start.6 = (s32[2]{0:T(128)S(1)}, s32[2]{0:T(128)}, u32[]{:S(2)}) copy-start(s32[2]{0:T(128)} %param.19) | copy-start | bytes 28
  122.2 41.3 %copy-start.5 = (s32[4,16]{1,0:T(4,128)S(1)}, s32[4,16]{1,0:T(4,128)}, u32[]{:S(2)}) copy-start(s32[4,16]{1,0:T(4,128)} %param.17) | copy-start | bytes 772
  122.2 41.5 %copy-start.7 = (s32[4]{0:T(128)S(1)}, s32[4]{0:T(128)}, u32[]{:S(2)}) copy-start(s32[4]{0:T(128)} %param.18) | copy-start | bytes 52
  129.7 167.8 %all-gather.10.cloned.1.call-start = ((), (), s32[]{:S(2)}) async-start(), calls=%async_computation.5 | async-start | bytes 4456448 | tf_op jit(solution)/shard_map/all_gather | solution.py:127
  130.5 179.8 %all-gather.12.cloned.1.call-start = ((), (), s32[]{:S(2)}) async-start(), calls=%async_computation.6 | async-start | bytes 4456448 | tf_op jit(solution)/shard_map/all_gather | solution.py:128
  131.0 229.9 %all-gather.14.cloned.1.call-start = ((), (), s32[]{:S(2)}) async-start(), calls=%async_computation.7 | async-start | bytes 4456448 | tf_op jit(solution)/shard_map/all_gather | solution.py:178
  230.9 38.0 %all-to-all-start.2 = ((f32[16,1,1024]{2,1,0:T(1,128)}), f32[16,1,1024]{2,1,0:T(1,128)S(1)}, u32[]{:S(2)}, u32[]{:S(2)}) async-start(f32[16,1,1024]{2,1,0:T(1,128)} %reshape.384), calls=%async_computation.2 | async-start | bytes 131072 | tf_op jit(solution)/shard_map/all_to_all | solution.py:148
  268.9 19.8 %all-to-all-start.1 = ((f32[16,1,1024]{2,1,0:T(1,128)}), f32[16,1,1024]{2,1,0:T(1,128)S(1)}, u32[]{:S(2)}, u32[]{:S(2)}) async-start(f32[16,1,1024]{2,1,0:T(1,128)} %reshape.386), calls=%async_computation.1 | async-start | bytes 131072 | tf_op jit(solution)/shard_map/all_to_all | solution.py:149
  282.5 14.9 %copy-start.1 = (bf16[2,64,1024]{2,1,0:T(8,128)(2,1)S(1)}, bf16[2,64,1024]{2,1,0:T(8,128)(2,1)}, u32[]{:S(2)}) copy-start(bf16[2,64,1024]{2,1,0:T(8,128)(2,1)} %get-tuple-element.278) | copy-start | bytes 786436
  288.8 61.7 %all-to-all-start = ((bf16[1,2,1024,1024]{3,1,0,2:T(2,128)(2,1)}), bf16[1,2,1024,1024]{3,1,0,2:T(2,128)(2,1)}, u32[]{:S(2)}, u32[]{:S(2)}) async-start(bf16[1,2,1024,1024]{3,1,0,2:T(2,128)(2,1)} %copy.101), calls=%async_computation | async-start | bytes 8388608 | tf_op jit(solution)/shard_map/all_to_all | solution.py:146
  350.5 10.4 %copy-start = (bf16[2,64,2048]{2,1,0:T(8,128)(2,1)S(1)}, bf16[2,64,2048]{2,1,0:T(8,128)(2,1)}, u32[]{:S(2)}) copy-start(bf16[2,64,2048]{2,1,0:T(8,128)(2,1)} %param.11) | copy-start | bytes 1572868
  360.0 4.2 %copy-start.3 = (f32[2048]{0:T(1024)S(1)}, f32[2048]{0:T(1024)}, u32[]{:S(2)}) copy-start(f32[2048]{0:T(1024)} %param.15) | copy-start | bytes 24580
  360.1 4.2 %copy-start.4 = (f32[2048]{0:T(1024)S(1)}, f32[2048]{0:T(1024)}, u32[]{:S(2)}) copy-start(f32[2048]{0:T(1024)} %param.14) | copy-start | bytes 24580
Sparse Core Ops, SparseCore 0:
  43.7 78.4 all-gather.5
  129.8 38.7 all-gather.7
  170.3 37.3 all-gather.9
  209.8 37.1 all-gather.11
  248.6 38.3 all-gather.13
where the time goes:
time: 376 us; the launch traced here: 372 us
  local copies, waits for them, and re-layouts  94.5 us (25%)
  waiting for transfers between devices  89.8 us (24%)
  blocking collectives  68.6 us (18%)
  matrix products  38.6 us (10%)
  other arithmetic  36.7 us (10%)
  starting transfers between devices  21.9 us (6%)
  between operations  14.5 us (4%)
  loops' own time  7.52 us (2%)
    all_gather x1, waiting for transfers between devices, body(): lax.all_gather(qkv_cols, 'fsdp', axis=0, tiled=True)  78.5 us
    all_gather x1, blocking collectives, body(): lax.all_gather(w_qkv, 'dp', axis=1, tiled=True)  36.4 us
    all_gather x1, blocking collectives, body(): lax.all_gather(w_out, 'dp', axis=1, tiled=True)  32.2 us
    unnamed x32, local copies, waits for them, and re-layouts  20.5 us
    dot_general x5, matrix products, one_block(): jnp.einsum('nhk,khd->nhd', expo.astype(jnp.bfloat16), value_rows, preferr...  17.8 us
    div x2, local copies, waits for them, and re-layouts, body(): owner_sum / jnp.maximum(owner_total, 1.0)[:, :, None]  15.7 us
    mul x2, local copies, waits for them, and re-layouts, body(): normed_parts.astype(jnp.float32) * factor[..., None]  15.5 us
    reduce_sum x5, other arithmetic, one_block(): row_total = jnp.sum(expo, axis=2)  12.5 us
  transfers between devices with their start and end apart: 8, of which 3 were waited for; matrix products, arithmetic and copies ran while one was open for 42% of the time, Pallas kernels for 0%

commit v1 on v0

v1 whole, which is shorter than its diff:
```python
import functools
import math

import jax
import jax.numpy as jnp
from jax import lax
from jax.experimental import pallas as pl
from jax.experimental.pallas import tpu as pltpu
from jax.sharding import PartitionSpec as P

HD = 128
NEG = -1e30
LN_EPS = 1e-06
LOG2E = 1.4426950408889634

NN = (((1,), (0,)), ((), ()))
NT = (((1,), (1,)), ((), ()))
TN = (((0,), (0,)), ((), ()))


def dot32(a, b, dims):
    return lax.dot_general(a, b, dims, preferred_element_type=jnp.float32)


def fold8(x, op):
    out = x[0:8]
    for i in range(1, x.shape[0] // 8):
        out = op(out, x[8 * i : 8 * i + 8])
    return out


def attention_kernel(
    half_slots,
    page_table,
    prefix_len,
    group_of,
    q_ref,
    kn_ref,
    vn_ref,
    pool_ref,
    o1_ref,
    s1_ref,
    o2_ref,
    s2_ref,
    sc,
    scn,
    m_ref,
    l_ref,
    acc,
    slot_list,
    base_list,
):
    y = lax.axis_index("fsdp") // 8
    rows = q_ref.shape[1]
    page = pool_ref.shape[1]
    n_pages = page_table.shape[1]
    inv_root = 1.0 / math.sqrt(HD)
    key_iota = lax.broadcasted_iota(jnp.int32, (page, rows), 0)
    for j in range(2):
        req = y if j == 0 else 1 - y
        group = group_of[req]
        length = prefix_len[group]

        def build(p, count):
            loc = page_table[group, p] - half_slots * y
            live = (loc >= 0) & (loc < half_slots) & (p * page < length)

            @pl.when(live)
            def _():
                slot_list[count] = loc
                base_list[count] = p * page

            return count + live.astype(jnp.int32)

        count = lax.fori_loop(0, n_pages, build, jnp.int32(0))
        m_ref[...] = jnp.full(m_ref.shape, NEG, jnp.float32)
        l_ref[...] = jnp.zeros(l_ref.shape, jnp.float32)
        acc[...] = jnp.zeros(acc.shape, jnp.float32)
        q = q_ref[j]

        @pl.loop(0, count)
        def _(i):
            keys = pool_ref[slot_list[i], :, :HD]
            s = dot32(keys, q, NT) * inv_root
            s = jnp.where(key_iota < length - base_list[i], s, NEG)
            sc[i] = s
            m_ref[...] = jnp.maximum(m_ref[...], fold8(s, jnp.maximum))

        if j == 0:
            for kb in range(rows // page):
                lo = kb * page
                s = dot32(kn_ref[lo : lo + page, :], q[lo:, :], NT) * inv_root
                ki = lax.broadcasted_iota(jnp.int32, s.shape, 0)
                qi = lax.broadcasted_iota(jnp.int32, s.shape, 1)
                s = jnp.where(ki <= qi, s, NEG)
                scn[kb, :, lo:] = s
                m_ref[:, lo:] = jnp.maximum(m_ref[:, lo:], fold8(s, jnp.maximum))
        top = jnp.max(m_ref[...], axis=0, keepdims=True)

        @pl.loop(0, count)
        def _(i):
            e = jnp.exp2((sc[i] - top) * LOG2E)
            l_ref[...] += fold8(e, jnp.add)
            values = pool_ref[slot_list[i], :, HD:]
            acc[...] += dot32(values, e.astype(jnp.bfloat16), TN)

        if j == 0:
            for kb in range(rows // page):
                lo = kb * page
                e = jnp.exp2((scn[kb, :, lo:] - top[:, lo:]) * LOG2E)
                l_ref[:, lo:] += fold8(e, jnp.add)
                acc[:, lo:] += dot32(vn_ref[lo : lo + page, :], e.astype(jnp.bfloat16), TN)
        total = jnp.sum(l_ref[...], axis=0, keepdims=True)
        if j == 0:
            o1_ref[...] = acc[...]
            s1_ref[0:1, :] = top
            s1_ref[1:2, :] = total
            s1_ref[2:8, :] = jnp.zeros((6, rows), jnp.float32)
        else:
            o2_ref[...] = (acc[...] / jnp.maximum(total, 1.0)).astype(jnp.bfloat16)
            s2_ref[0:1, :] = top
            s2_ref[1:2, :] = total
            s2_ref[2:8, :] = jnp.zeros((6, rows), jnp.float32)


def attention(page_table, prefix_len, group_of, q2, k_new, v_new, pool):
    rows = q2.shape[1]
    slots, page = pool.shape[0], pool.shape[1]
    smem = pl.BlockSpec(memory_space=pltpu.SMEM)
    vmem = pl.BlockSpec(memory_space=pltpu.VMEM)
    return pl.pallas_call(
        functools.partial(attention_kernel, slots),
        out_shape=(
            jax.ShapeDtypeStruct((HD, rows), jnp.float32),
            jax.ShapeDtypeStruct((8, rows), jnp.float32),
            jax.ShapeDtypeStruct((HD, rows), jnp.bfloat16),
            jax.ShapeDtypeStruct((8, rows), jnp.float32),
        ),
        in_specs=[smem, smem, smem, vmem, vmem, vmem, vmem],
        out_specs=(vmem, vmem, vmem, vmem),
        scratch_shapes=[
            pltpu.VMEM((page_table.shape[1], page, rows), jnp.float32),
            pltpu.VMEM((rows // page, page, rows), jnp.float32),
            pltpu.VMEM((8, rows), jnp.float32),
            pltpu.VMEM((8, rows), jnp.float32),
            pltpu.VMEM((HD, rows), jnp.float32),
            pltpu.SMEM((page_table.shape[1],), jnp.int32),
            pltpu.SMEM((page_table.shape[1],), jnp.int32),
        ],
        compiler_params=pltpu.CompilerParams(vmem_limit_bytes=48 << 20),
        name="attend",
    )(page_table, prefix_len, group_of, q2, k_new, v_new, pool)


def body(tokens, w_qkv, w_out, ln_gain, ln_bias, kv_pool, page_table, prefix_len, group_of):
    reqs, toks, width = tokens.shape
    owners = lax.axis_size("fsdp")
    heads = owners // 2
    inner = heads * HD
    f = lax.axis_index("fsdp")
    y = f // heads
    rows = toks * owners
    rowsets = [list(range(heads)), list(range(heads, 2 * heads))]
    flip = [(i, (i + heads) % owners) for i in range(owners)]

    wall = lax.all_gather(w_qkv, "dp", axis=1, tiled=True)
    wh = wall.reshape(wall.shape[0], 3, heads, HD).transpose(2, 0, 1, 3)
    wh = wh.reshape(1, heads, wall.shape[0], 3 * HD)
    wh = jnp.concatenate([wh, wh], 0).reshape(owners, wall.shape[0], 3 * HD)
    wh = lax.all_to_all(wh, "fsdp", 0, 0, tiled=True).reshape(width, 3 * HD)
    sent = jnp.repeat(tokens, heads, axis=0)
    mine = lax.all_to_all(sent, "fsdp", 0, 0, tiled=True).reshape(rows, width)
    qkv = jnp.dot(mine, wh, preferred_element_type=jnp.float32).astype(jnp.bfloat16)
    q, k, v = qkv[:, :HD], qkv[:, HD : 2 * HD], qkv[:, 2 * HD :]

    kv = lax.all_to_all(
        qkv[:, HD:].reshape(owners, toks, 2 * HD), "fsdp", 0, 0, tiled=True
    )
    new_cache = (
        kv.reshape(2, heads, toks, 2, HD).transpose(0, 2, 3, 1, 4).reshape(2, toks, 2 * inner)
    )
    slots, page = kv_pool.shape[0], kv_pool.shape[1]
    ps = kv_pool.reshape(slots, page, 2, heads, HD).transpose(3, 0, 1, 2, 4)
    ps = lax.all_to_all(
        ps.reshape(heads, slots, page, 2 * HD), "fsdp", 0, 0, axis_index_groups=rowsets, tiled=True
    )
    pool = ps.reshape(heads * slots, page, 2 * HD)
    q_par = lax.ppermute(q, "fsdp", flip)
    o1, s1, o2, s2 = attention(
        page_table, prefix_len, group_of, jnp.stack([q, q_par]), k, v, pool
    )
    o2, s2 = lax.ppermute(o2, "fsdp", flip), lax.ppermute(s2, "fsdp", flip)
    top = jnp.maximum(s1[0], s2[0])
    f1 = jnp.exp(s1[0] - top)
    f2 = jnp.exp(s2[0] - top) * s2[1]
    attn = (o1 * f1 + o2.astype(jnp.float32) * f2) / (s1[1] * f1 + f2)
    attn = attn.T.astype(jnp.bfloat16).reshape(owners, toks, HD)
    attn = lax.all_to_all(attn, "fsdp", 0, 0, tiled=True)
    attn = attn.reshape(2, heads, toks, HD).transpose(0, 2, 1, 3).reshape(2 * toks, inner)

    wo = lax.all_gather(lax.all_gather(w_out, "dp", axis=1, tiled=True), "fsdp", axis=0, tiled=True)
    proj = jnp.dot(attn, wo, preferred_element_type=jnp.float32)
    mixed = tokens.reshape(reqs * toks, width).astype(jnp.float32) + proj
    centred = mixed - jnp.mean(mixed, axis=1, keepdims=True)
    var = jnp.mean(centred * centred, axis=1, keepdims=True)
    normed = centred * lax.rsqrt(var + LN_EPS) * ln_gain[None, :] + ln_bias[None, :]
    return normed.astype(jnp.bfloat16).reshape(reqs, toks, width), new_cache


def solution(mesh):
    in_specs = (
        P("dp", "fsdp", None),
        P("fsdp", "dp"),
        P("fsdp", "dp"),
        P(),
        P(),
        P("fsdp", None, None),
        P(),
        P(),
        P("dp"),
    )
    out_specs = (P("dp", "fsdp", None), P("dp", "fsdp", None))
    return jax.shard_map(body, mesh=mesh, in_specs=in_specs, out_specs=out_specs, check_vma=False)
```

time: 376 us -> 266 us (0.71)
  local copies, waits for them, and re-layouts: 94.5 us -> 15.4 us
  other arithmetic: 36.7 us -> 1.63 us
  matrix products: 38.6 us -> 8 us
  starting transfers between devices: 21.9 us -> 45.9 us
  loops' own time: 7.52 us -> 0 us
  waiting for transfers between devices: 89.8 us -> 96.8 us
  blocking collectives: 68.6 us -> 74.9 us
  Pallas kernels: 0 us -> 6.24 us
    all_to_all x3 -> x5, waiting for transfers between devices: 8.28 us -> 89.7 us  [the longest x1 63.8 us: body(): mine = lax.all_to_all(sent, 'fsdp', 0, 0, tiled=True).reshape(rows, width)]
    all_gather x5 -> x1, waiting for transfers between devices: 80.2 us -> 0.02 us  [body(): lax.all_gather(lax.all_gather(w_out, 'dp', axis=1, tiled=True), 'fsdp', a...]
    dot_general x12 -> x2, matrix products: 38.6 us -> 8 us  [the longest x1 4.99 us: body(): jnp.dot(mine, wh, preferred_element_type=jnp.float32).astype(jnp.bfloat16)]
    reduce_sum x10 -> x1, other arithmetic: 22.7 us -> 0.26 us  [body(): var = jnp.mean(centred * centred, axis=1, keepdims=True)]
    all_to_all x3 -> x5, starting transfers between devices: 21.7 us -> 42.3 us  [the longest x1 16.8 us: body(): mine = lax.all_to_all(sent, 'fsdp', 0, 0, tiled=True).reshape(rows, width)]
    unnamed x32 -> x30, local copies, waits for them, and re-layouts: 20.5 us -> 2.47 us
    mul x4 -> x0, local copies, waits for them, and re-layouts: 16.3 us -> none  [the longest x2 15.5 us: body(): normed_parts.astype(jnp.float32) * factor[..., None]]
    div x3 -> x0, local copies, waits for them, and re-layouts: 15.9 us -> none  [the longest x2 15.7 us: body(): owner_sum / jnp.maximum(owner_total, 1.0)[:, :, None]]
  transfers between devices with their start and end apart: 8 -> 9, of which waited for: 3 -> 6; matrix products, arithmetic and copies ran while one was open for 42% -> 6% of each run, Pallas kernels for 0% -> 2%
where the time goes in v1:
time: 266 us; the launch traced here: 263 us
  waiting for transfers between devices  96.8 us (36%)
  blocking collectives  74.9 us (28%)
  starting transfers between devices  45.9 us (17%)
  local copies, waits for them, and re-layouts  15.4 us (6%)
  between operations  14.3 us (5%)
  matrix products  8 us (3%)
  Pallas kernels  6.24 us (2%)
    all_to_all x1, waiting for transfers between devices, body(): mine = lax.all_to_all(sent, 'fsdp', 0, 0, tiled=True).reshape(rows, width)  63.8 us
    all_gather x1, blocking collectives, body(): lax.all_gather(w_out, 'dp', axis=1, tiled=True)  41.2 us
    all_gather x1, blocking collectives, body(): wall = lax.all_gather(w_qkv, 'dp', axis=1, tiled=True)  33.7 us
    all_to_all x1, starting transfers between devices, body(): mine = lax.all_to_all(sent, 'fsdp', 0, 0, tiled=True).reshape(rows, width)  16.8 us
    all_to_all x1, waiting for transfers between devices, body(): lax.all_to_all(ps.reshape(heads, slots, page, 2 * HD), 'fsdp', 0, 0, axis...  12.2 us
    all_to_all x1, starting transfers between devices, body(): wh = lax.all_to_all(wh, 'fsdp', 0, 0, tiled=True).reshape(width, 3 * HD)  11.4 us
    all_to_all x1, waiting for transfers between devices, body(): lax.all_to_all(qkv[:, HD:].reshape(owners, toks, 2 * HD), 'fsdp', 0, 0, t...  8.2 us
    ppermute x1, waiting for transfers between devices, body(): q_par = lax.ppermute(q, 'fsdp', flip)  6.68 us
  transfers between devices with their start and end apart: 9, of which 6 were waited for; matrix products, arithmetic and copies ran while one was open for 6% of the time, Pallas kernels for 2%

profile of v1, /device:TPU:1, one launch (start us, length us, event | category | flops | bytes accessed | tf_op | source)
XLA Modules:
  0.0 263.1 jit_solution(4811175975081025488)
XLA Ops:
  7.2 1.0 copy.19
  8.2 33.7 %all_gather.9 = bf16[128,3072]{0,1:T(8,128)(2,1)S(1)} all-gather(bf16[128,384]{0,1:T(8,128)(2,1)S(1)} %copy.19), channel_id=1, replica_groups=mesh['dp'=8,'fsdp'=16] {'dp'}, dimensions={1}, use_global_device_ids=true | all-gather | bytes 884736 | tf_op jit(solution)/shard_map/all_gather | solution.py:166
  41.9 0.1 copy.20
  42.0 0.1 pad_maximum_fusion
  42.1 1.6 copy.21
  43.7 11.4 %all-to-all-start = ((bf16[16,128,384]{2,1,0:T(8,128)(2,1)}), bf16[16,128,384]{2,1,0:T(8,128)(2,1)S(1)}, u32[]{:S(2)}, u32[]{:S(2)}) async-start(bf16[16,128,384]{2,1,0:T(8,128)(2,1)} %copy.21), calls=%async_computation | async-start | bytes 3145728 | tf_op jit(solution)/shard_map/all_to_all | solution.py:170
  55.2 0.0 all-gather.2.cloned.1.call-start
  55.2 41.2 %all_gather.10 = bf16[64,2048]{1,0:T(8,128)(2,1)} all-gather(bf16[64,256]{1,0:T(8,128)(2,1)S(1)} %copy-done.11), channel_id=1, replica_groups=mesh['dp'=8,'fsdp'=16] {'dp'}, dimensions={1}, use_global_device_ids=true | all-gather | bytes 294912 | tf_op jit(solution)/shard_map/all_gather | solution.py:201
  96.4 0.0 all-gather.2.cloned.1.call-update
  96.5 2.5 broadcast_in_dim.2
  99.0 16.8 %all-to-all-start.1 = ((bf16[16,64,2048]{2,1,0:T(8,128)(2,1)}), bf16[16,64,2048]{2,1,0:T(8,128)(2,1)}, u32[]{:S(2)}, u32[]{:S(2)}) async-start(bf16[16,64,2048]{2,1,0:T(8,128)(2,1)} %bitcast.48), calls=%async_computation.1 | async-start | bytes 8388608 | tf_op jit(solution)/shard_map/all_to_all | solution.py:172
  115.8 0.6 copy.28
  116.5 2.2 copy.23
  118.7 2.7 %reshape.76 = bf16[8,4,128,256]{3,2,1,0:T(8,128)(2,1)} reshape(bf16[8,4,128,2,128]{4,3,2,1,0:T(2,128)(2,1)S(1)} %copy.23) | data formatting | bytes 4194304 | tf_op jit(solution)/shard_map/reshape | solution.py:185
  121.4 63.8 %all-to-all-done.1 = bf16[16,64,2048]{2,1,0:T(8,128)(2,1)} async-done(((bf16[16,64,2048]{2,1,0:T(8,128)(2,1)}), bf16[16,64,2048]{2,1,0:T(8,128)(2,1)}, u32[]{:S(2)}, u32[]{:S(2)}) %all-to-all-start.1) | async-done | bytes 4194336 | tf_op jit(solution)/shard_map/all_to_all | solution.py:172
  185.2 4.3 %all-to-all-start.2 = ((bf16[8,4,128,256]{3,2,1,0:T(8,128)(2,1)}), bf16[8,4,128,256]{3,2,1,0:T(8,128)(2,1)S(1)}, u32[]{:S(2)}, u32[]{:S(2)}) async-start(bf16[8,4,128,256]{3,2,1,0:T(8,128)(2,1)} %reshape.76), calls=%async_computation.2 | async-start | bytes 4194304 | tf_op jit(solution)/shard_map/all_to_all | solution.py:184
  189.5 5.0 %fusion = bf16[1024,384]{1,0:T(8,128)(2,1)S(1)} fusion(bf16[1024,2048]{1,0:T(8,128)(2,1)} %bitcast.7, bf16[2048,384]{1,0:T(8,128)(2,1)} %bitcast.56), kind=kOutput, calls=%fused_computation.3 | convolution fusion | flops 1611005952 | bytes 6553600 | tf_op jit(solution)/shard_map/dot_general | solution.py:173
  194.5 0.0 copy-start.2
  194.5 0.0 copy-start.3
  194.5 0.0 copy-start.4
  194.5 0.2 fusion.9
  194.7 2.1 collective-permute-start
  196.8 6.7 %collective-permute-done = bf16[1024,128]{1,0:T(8,128)(2,1)S(1)} collective-permute-done((bf16[1024,128]{1,0:T(8,128)(2,1)S(1)}, bf16[1024,128]{1,0:T(8,128)(2,1)S(1)}, u32[]{:S(2)}, u32[]{:S(2)}) %collective-permute-start) | collective-permute-done | bytes 262176 | tf_op jit(solution)/shard_map/ppermute | solution.py:188
  203.5 0.1 pad_maximum_fusion.1.q_ref
  203.5 12.2 %all-to-all-done.2 = bf16[8,4,128,256]{3,2,1,0:T(8,128)(2,1)S(1)} async-done(((bf16[8,4,128,256]{3,2,1,0:T(8,128)(2,1)}), bf16[8,4,128,256]{3,2,1,0:T(8,128)(2,1)S(1)}, u32[]{:S(2)}, u32[]{:S(2)}) %all-to-all-start.2) | async-done | bytes 2097184 | tf_op jit(solution)/shard_map/all_to_all | solution.py:184
  215.7 6.2 %attend.1 = (f32[128,1024]{1,0:T(8,128)S(1)}, f32[8,1024]{1,0:T(8,128)S(1)}, bf16[128,1024]{1,0:T(8,128)(2,1)S(1)}, f32[8,1024]{1,0:T(8,128)S(1)}) custom-call(s32[4,16]{1,0:T(4,128)S(1)} %copy-done.2, s32[4]{0:T(128)S(1)} %copy-done.3, s32[2]{0:T(128)S(1)} %copy-done.4, bf16[2,1024,128]{2,1,0:T(8,128)(2,1)S(1)} %pad_maximum_fusion.1.q_ref, ...), custom_call_target="tpu_custom_call" | custom-call | tf_op jit(solution)/shard_map/attend/pallas_call | solution.py:131
  222.0 0.0 copy-start
  222.0 0.8 copy-done
  222.8 0.0 collective-permute-start.2
  222.8 1.4 collective-permute-start.1
  224.2 0.8 slice.39
  225.1 4.9 %all-to-all-start.4 = ((bf16[16,64,256]{2,1,0:T(8,128)(2,1)}), bf16[16,64,256]{2,1,0:T(8,128)(2,1)S(1)}, u32[]{:S(2)}, u32[]{:S(2)}) async-start(bf16[16,64,256]{2,1,0:T(8,128)(2,1)} %bitcast.21), calls=%async_computation.4 | async-start | bytes 1048576 | tf_op jit(solution)/shard_map/all_to_all | solution.py:176
  230.0 0.4 collective-permute-done.1
  230.4 0.1 fusion.3
  230.5 0.8 copy.24
  231.3 8.2 %all-to-all-done.4 = bf16[16,64,256]{2,1,0:T(8,128)(2,1)S(1)} async-done(((bf16[16,64,256]{2,1,0:T(8,128)(2,1)}), bf16[16,64,256]{2,1,0:T(8,128)(2,1)S(1)}, u32[]{:S(2)}, u32[]{:S(2)}) %all-to-all-start.4) | async-done | bytes 524320 | tf_op jit(solution)/shard_map/all_to_all | solution.py:176
  239.6 4.9 %all-to-all-start.3 = ((bf16[16,64,128]{2,1,0:T(8,128)(2,1)}), bf16[16,64,128]{2,1,0:T(8,128)(2,1)S(1)}, u32[]{:S(2)}, u32[]{:S(2)}) async-start(bf16[16,64,128]{2,1,0:T(8,128)(2,1)} %bitcast.17), calls=%async_computation.3 | async-start | bytes 524288 | tf_op jit(solution)/shard_map/all_to_all | solution.py:198
  244.4 0.1 reshape.83
  244.6 0.6 copy.37
  245.2 1.0 reshape.84
  246.2 5.5 %all-to-all-done.3 = bf16[16,64,128]{2,1,0:T(8,128)(2,1)S(1)} async-done(((bf16[16,64,128]{2,1,0:T(8,128)(2,1)}), bf16[16,64,128]{2,1,0:T(8,128)(2,1)S(1)}, u32[]{:S(2)}, u32[]{:S(2)}) %all-to-all-start.3) | async-done | bytes 262176 | tf_op jit(solution)/shard_map/all_to_all | solution.py:198
  251.7 0.2 copy.25
  251.9 0.0 all-gather.2.cloned.1.call-done
  251.9 0.0 copy-start.12
  251.9 0.0 copy-start.13
  251.9 3.0 %fusion.10 = (f32[128]{0:T(128)S(1)}, f32[128,2048]{1,0:T(8,128)S(1)}) fusion(bf16[1024,2048]{1,0:T(8,128)(2,1)} %all-gather.2.cloned.1.call-done, bf16[16,8,8,128]{3,2,1,0:T(8,128)(2,1)S(1)} %bitcast.57, bf16[128,2048]{1,0:T(8,128)(2,1)S(1)} %bitcast.53), kind=kOutput, calls=%fused_computation.22 | convolution fusion | flops 537657216 | bytes 6029824 | tf_op jit(solution)/shard_map/dot_general | solution.py:202
  255.0 0.3 multiply_reduce_fusion
  255.2 1.0 add_convert_fusion
  (26 shorter events, 0.1 us)
Async XLA Ops:
  43.7 11.5 %copy-start.11 = (bf16[64,256]{1,0:T(8,128)(2,1)S(1)}, bf16[64,256]{1,0:T(8,128)(2,1)}, u32[]{:S(2)}) copy-start(bf16[64,256]{1,0:T(8,128)(2,1)} %param.11) | copy-start | bytes 98308
  43.7 52.7 %copy-start.7 = (bf16[2,64,2048]{2,1,0:T(8,128)(2,1)S(1)}, bf16[2,64,2048]{2,1,0:T(8,128)(2,1)}, u32[]{:S(2)}) copy-start(bf16[2,64,2048]{2,1,0:T(8,128)(2,1)} %param.9) | copy-start | bytes 1572868
  43.7 52.7 %all-to-all-start = ((bf16[16,128,384]{2,1,0:T(8,128)(2,1)}), bf16[16,128,384]{2,1,0:T(8,128)(2,1)S(1)}, u32[]{:S(2)}, u32[]{:S(2)}) async-start(bf16[16,128,384]{2,1,0:T(8,128)(2,1)} %copy.21), calls=%async_computation | async-start | bytes 3145728 | tf_op jit(solution)/shard_map/all_to_all | solution.py:170
  55.2 196.7 %all-gather.2.cloned.1.call-start = ((), (), s32[]{:S(2)}) async-start(), calls=%async_computation.5 | async-start | bytes 4456448 | tf_op jit(solution)/shard_map/all_gather | solution.py:201
  96.5 2.6 copy-start.10
  99.0 16.8 %copy-start.9 = (bf16[4,128,2048]{2,1,0:T(8,128)(2,1)S(1)}, bf16[4,128,2048]{2,1,0:T(8,128)(2,1)}, u32[]{:S(2)}) copy-start(bf16[4,128,2048]{2,1,0:T(8,128)(2,1)} %param.14) | copy-start | bytes 6291460
  99.0 86.2 %all-to-all-start.1 = ((bf16[16,64,2048]{2,1,0:T(8,128)(2,1)}), bf16[16,64,2048]{2,1,0:T(8,128)(2,1)}, u32[]{:S(2)}, u32[]{:S(2)}) async-start(bf16[16,64,2048]{2,1,0:T(8,128)(2,1)} %bitcast.48), calls=%async_computation.1 | async-start | bytes 8388608 | tf_op jit(solution)/shard_map/all_to_all | solution.py:172
  185.2 30.5 %all-to-all-start.2 = ((bf16[8,4,128,256]{3,2,1,0:T(8,128)(2,1)}), bf16[8,4,128,256]{3,2,1,0:T(8,128)(2,1)S(1)}, u32[]{:S(2)}, u32[]{:S(2)}) async-start(bf16[8,4,128,256]{3,2,1,0:T(8,128)(2,1)} %reshape.76), calls=%async_computation.2 | async-start | bytes 4194304 | tf_op jit(solution)/shard_map/all_to_all | solution.py:184
  194.5 9.0 %copy-start.5 = (bf16[1024,384]{1,0:T(8,128)(2,1)}, bf16[1024,384]{1,0:T(8,128)(2,1)S(1)}, u32[]{:S(2)}) copy-start(bf16[1024,384]{1,0:T(8,128)(2,1)S(1)} %fusion) | copy-start | bytes 2359300
  194.5 21.2 %copy-start.2 = (s32[4,16]{1,0:T(4,128)S(1)}, s32[4,16]{1,0:T(4,128)}, u32[]{:S(2)}) copy-start(s32[4,16]{1,0:T(4,128)} %page_table.1) | copy-start | bytes 772
  194.5 21.2 %copy-start.3 = (s32[4]{0:T(128)S(1)}, s32[4]{0:T(128)}, u32[]{:S(2)}) copy-start(s32[4]{0:T(128)} %prefix_len.1) | copy-start | bytes 52
  194.5 21.2 %copy-start.4 = (s32[2]{0:T(128)S(1)}, s32[2]{0:T(128)}, u32[]{:S(2)}) copy-start(s32[2]{0:T(128)} %group_of.1) | copy-start | bytes 28
  194.7 8.8 %collective-permute-start = (bf16[1024,128]{1,0:T(8,128)(2,1)S(1)}, bf16[1024,128]{1,0:T(8,128)(2,1)S(1)}, u32[]{:S(2)}, u32[]{:S(2)}) collective-permute-start(bf16[1024,128]{1,0:T(8,128)(2,1)S(1)} %get-tuple-element.16), channel_id=1, source_target_pairs={{0,8},{1,9},{2,10},{3,11},{4,12},{5,13},{6,14},{7,15},{8,0},{9,1},... | collective-permute-start | bytes 786440 | tf_op jit(solution)/shard_map/ppermute | solution.py:188
  215.7 8.5 %copy-start.6 = (bf16[1024,384]{1,0:T(8,128)(2,1)S(1)}, bf16[1024,384]{1,0:T(8,128)(2,1)}, u32[]{:S(2)}) copy-start(bf16[1024,384]{1,0:T(8,128)(2,1)} %copy-done.5) | copy-start | bytes 2359300
  222.0 0.8 copy-start
  222.8 7.6 %copy-start.1 = (f32[128,1024]{1,0:T(8,128)S(1)}, f32[128,1024]{1,0:T(8,128)}, u32[]{:S(2)}) copy-start(f32[128,1024]{1,0:T(8,128)} %copy-done) | copy-start | bytes 1572868
  222.8 7.6 %collective-permute-start.2 = (bf16[128,1024]{1,0:T(8,128)(2,1)S(1)}, bf16[128,1024]{1,0:T(8,128)(2,1)S(1)}, u32[]{:S(2)}, u32[]{:S(2)}) collective-permute-start(bf16[128,1024]{1,0:T(8,128)(2,1)S(1)} %get-tuple-element.9), channel_id=1, source_target_pairs={{0,8},{1,9},{2,10},{3,11},{4,12},{5,13},{6,14},{7,15},{8,0},{9,1},... | collective-permute-start | bytes 786440 | tf_op jit(solution)/shard_map/ppermute | solution.py:192
  222.8 7.6 %collective-permute-start.1 = (f32[8,1024]{1,0:T(8,128)S(1)}, f32[8,1024]{1,0:T(8,128)S(1)}, u32[]{:S(2)}, u32[]{:S(2)}) collective-permute-start(f32[8,1024]{1,0:T(8,128)S(1)} %get-tuple-element.8), channel_id=1, source_target_pairs={{0,8},{1,9},{2,10},{3,11},{4,12},{5,13},{6,14},{7,15},{8,0},{9,1},... | collective-permute-start | bytes 98312 | tf_op jit(solution)/shard_map/ppermute | solution.py:192
  225.1 14.5 %all-to-all-start.4 = ((bf16[16,64,256]{2,1,0:T(8,128)(2,1)}), bf16[16,64,256]{2,1,0:T(8,128)(2,1)S(1)}, u32[]{:S(2)}, u32[]{:S(2)}) async-start(bf16[16,64,256]{2,1,0:T(8,128)(2,1)} %bitcast.21), calls=%async_computation.4 | async-start | bytes 1048576 | tf_op jit(solution)/shard_map/all_to_all | solution.py:176
  239.6 12.3 %copy-start.8 = (bf16[2,64,2048]{2,1,0:T(8,128)(2,1)S(1)}, bf16[2,64,2048]{2,1,0:T(8,128)(2,1)}, u32[]{:S(2)}) copy-start(bf16[2,64,2048]{2,1,0:T(8,128)(2,1)} %param.9) | copy-start | bytes 1572868
  239.6 12.1 %all-to-all-start.3 = ((bf16[16,64,128]{2,1,0:T(8,128)(2,1)}), bf16[16,64,128]{2,1,0:T(8,128)(2,1)S(1)}, u32[]{:S(2)}, u32[]{:S(2)}) async-start(bf16[16,64,128]{2,1,0:T(8,128)(2,1)} %bitcast.17), calls=%async_computation.3 | async-start | bytes 524288 | tf_op jit(solution)/shard_map/all_to_all | solution.py:198
  251.9 3.3 %copy-start.12 = (f32[2048]{0:T(1024)S(1)}, f32[2048]{0:T(1024)}, u32[]{:S(2)}) copy-start(f32[2048]{0:T(1024)} %param.13) | copy-start | bytes 24580
  251.9 3.3 %copy-start.13 = (f32[2048]{0:T(1024)S(1)}, f32[2048]{0:T(1024)}, u32[]{:S(2)}) copy-start(f32[2048]{0:T(1024)} %param.12) | copy-start | bytes 24580
Sparse Core Ops, SparseCore 0:
  96.6 89.2 all-gather.1

commit v2 on v1

--- a/solution.py
+++ b/solution.py
@@ -152,42 +152,295 @@
     )(page_table, prefix_len, group_of, q2, k_new, v_new, pool)
 
 
+MESH = pl.DeviceIdType.MESH
+
+
+class Copies:
+    def __init__(self):
+        self.started = []
+
+    def send(self, src, dst, send_sem, recv_sem, device_id):
+        copy = pltpu.make_async_remote_copy(
+            src_ref=src,
+            dst_ref=dst,
+            send_sem=send_sem,
+            recv_sem=recv_sem,
+            device_id=device_id,
+            device_id_type=MESH,
+        )
+        copy.start()
+        self.started.append(copy)
+
+    def finish(self):
+        for copy in self.started:
+            copy.wait_send()
+
+
+def await_copy(dst, recv_sem):
+    pltpu.make_async_copy(dst, dst, recv_sem).wait()
+
+
+def front_kernel(
+    tokens,
+    w_ref,
+    pool_in,
+    q2,
+    kv,
+    pool,
+    cache,
+    x_buf,
+    wall,
+    wh,
+    x_send,
+    x_recv,
+    w1_send,
+    w1_recv,
+    w2_send,
+    w2_recv,
+    w3_send,
+    w3_recv,
+    p_send,
+    p_recv,
+    c_send,
+    c_recv,
+    q_sem,
+    local_sem,
+):
+    d = lax.axis_index("dp")
+    f = lax.axis_index("fsdp")
+    planes, owners = 8, 16
+    heads = owners // 2
+    y, h = f // heads, lax.rem(f, heads)
+    x, core = h // 2, lax.rem(f, 2)
+    toks = tokens.shape[1]
+    wr = w_ref.shape[0]
+    slots = pool_in.shape[0]
+
+    def at(yy, xx, cc):
+        return (yy * 4 + lax.rem(xx, 4)) * 2 + cc
+
+    right, left = at(y, x + 1, core), at(y, x + 3, core)
+    across, twin = at(1 - y, x, core), at(y, x, 1 - core)
+
+    barrier = pltpu.get_barrier_semaphore()
+    for k in range(1, owners):
+        pl.semaphore_signal(
+            barrier, inc=1, device_id={"fsdp": lax.rem(f + k, owners)}, device_id_type=MESH
+        )
+    for k in range(1, planes):
+        pl.semaphore_signal(
+            barrier, inc=1, device_id={"dp": lax.rem(d + k, planes)}, device_id_type=MESH
+        )
+    own_w = pltpu.make_async_copy(w_ref, wall.at[d], local_sem.at[0])
+    own_w.start()
+    own_x = pltpu.make_async_copy(tokens.at[y], x_buf.at[f], local_sem.at[1])
+    own_x.start()
+    pl.semaphore_wait(barrier, owners + planes - 2)
+
+    out = Copies()
+    for k in range(1, planes):
+        out.send(
+            w_ref, wall.at[d], w1_send.at[k - 1], w1_recv.at[d], {"dp": lax.rem(d + k, planes)}
+        )
+
+    def send_x(n, src, who, dest):
+        out.send(src, x_buf.at[who], x_send.at[n], x_recv.at[who], {"fsdp": dest})
+
+    send_x(0, tokens.at[1 - y], f, across)
+    send_x(1, tokens.at[y], f, right)
+    send_x(2, tokens.at[y], f, left)
+    send_x(3, tokens.at[y], f, twin)
+
+    for s in range(planes):
+
+        @pl.when(d == s)
+        def _():
+            own_w.wait()
+
+        @pl.when(d != s)
+        def _():
+            await_copy(wall.at[s], w1_recv.at[s])
+
+        for j in range(3):
+            t, head = divmod(3 * s + j, heads)
+            src = wall.at[s, :, pl.ds(HD * j, HD)]
+            dst = wh.at[f, :, pl.ds(HD * t, HD)]
+
+            @pl.when(h == head)
+            def _():
+                pltpu.make_async_copy(src, dst, w2_recv.at[h, t]).start()
+
+            @pl.when(h != head)
+            def _():
+                pltpu.make_async_remote_copy(
+                    src_ref=src,
+                    dst_ref=dst,
+                    send_sem=w2_send.at[3 * s + j],
+                    recv_sem=w2_recv.at[h, t],
+                    device_id={"fsdp": y * heads + head},
+                    device_id_type=MESH,
+                ).start()
+
+    await_copy(x_buf.at[across], x_recv.at[across])
+    send_x(4, x_buf.at[across], across, right)
+    send_x(5, x_buf.at[across], across, left)
+    send_x(6, x_buf.at[across], across, twin)
+    a_left, b_left = at(y, x + 3, core), at(1 - y, x + 3, core)
+    a_right, b_right = at(y, x + 1, core), at(1 - y, x + 1, core)
+    a_far, b_far = at(y, x + 2, core), at(1 - y, x + 2, core)
+    await_copy(x_buf.at[a_left], x_recv.at[a_left])
+    send_x(7, x_buf.at[a_left], a_left, right)
+    send_x(8, x_buf.at[a_left], a_left, twin)
+    await_copy(x_buf.at[a_right], x_recv.at[a_right])
+    send_x(9, x_buf.at[a_right], a_right, twin)
+
+    for r in range(heads):
+        src = y * heads + r
+        for t in range(3):
+            part = wh.at[src, :, pl.ds(HD * t, HD)]
+            await_copy(part, w2_recv.at[r, t])
+        out.send(wh.at[src], wh.at[src], w3_send.at[r], w3_recv.at[r], {"fsdp": across})
+
+    await_copy(x_buf.at[b_right], x_recv.at[b_right])
+    send_x(10, x_buf.at[b_right], b_right, left)
+    send_x(11, x_buf.at[b_right], b_right, twin)
+    await_copy(x_buf.at[b_left], x_recv.at[b_left])
+    send_x(12, x_buf.at[b_left], b_left, twin)
+
+    own_pool = []
+    for k in range(heads):
+        head = lax.rem(h + k, heads)
+        for t in range(2):
+            cols = pl.ds(pl.multiple_of((t * heads + head) * HD, HD), HD)
+            src = pool_in.at[:, :, cols]
+            dst = pool.at[pl.ds(h * slots, slots), :, pl.ds(t * HD, HD)]
+            if k == 0:
+                copy = pltpu.make_async_copy(src, dst, local_sem.at[2 + t])
+                copy.start()
+                own_pool.append(copy)
+            else:
+                out.send(
+                    src, dst, p_send.at[k, t], p_recv.at[h, t], {"fsdp": y * heads + head}
+                )
+
+    await_copy(x_buf.at[a_far], x_recv.at[a_far])
+    send_x(13, x_buf.at[a_far], a_far, twin)
+    await_copy(x_buf.at[b_far], x_recv.at[b_far])
+    send_x(14, x_buf.at[b_far], b_far, twin)
+    for yy in range(2):
+        for xx in range(4):
+            who = at(yy, xx, 1 - core)
+            await_copy(x_buf.at[who], x_recv.at[who])
+    own_x.wait()
+    for r in range(heads):
+        src = (1 - y) * heads + r
+        await_copy(wh.at[src], w3_recv.at[r])
+
+    @pl.loop(0, owners // 4)
+    def _(i):
+        left_rows = x_buf[pl.ds(4 * i, 4)].reshape(4 * toks, owners * wr)
+        got = dot32(left_rows, wh[...].reshape(owners * wr, 3 * HD), NN).astype(jnp.bfloat16)
+        q2[0, pl.ds(pl.multiple_of(4 * i * toks, 4 * toks), 4 * toks), :] = got[:, :HD]
+        kv[pl.ds(4 * i, 4)] = got[:, HD:].reshape(4, toks, 2 * HD)
+
+    out.send(q2.at[0], q2.at[1], q_sem.at[0], q_sem.at[1], {"fsdp": across})
+    own_cache = []
+    for k in range(owners):
+        who = lax.rem(f + k, owners)
+        for t in range(2):
+            cols = pl.ds(pl.multiple_of((t * heads + h) * HD, HD), HD)
+            src = kv.at[who, :, pl.ds(t * HD, HD)]
+            dst = cache.at[y, :, cols]
+            if k == 0:
+                copy = pltpu.make_async_copy(src, dst, local_sem.at[4 + t])
+                copy.start()
+                own_cache.append(copy)
+            else:
+                out.send(src, dst, c_send.at[k, t], c_recv.at[f, t], {"fsdp": who})
+
+    await_copy(q2.at[1], q_sem.at[1])
+    for copy in own_pool + own_cache:
+        copy.wait()
+    for k in range(1, heads):
+        who = lax.rem(h + k, heads)
+        for t in range(2):
+            await_copy(
+                pool.at[pl.ds(who * slots, slots), :, pl.ds(t * HD, HD)], p_recv.at[who, t]
+            )
+    for k in range(1, owners):
+        who = lax.rem(f + k, owners)
+        for t in range(2):
+            cols = pl.ds(pl.multiple_of((t * heads + lax.rem(who, heads)) * HD, HD), HD)
+            await_copy(cache.at[who // heads, :, cols], c_recv.at[who, t])
+    for s in range(planes):
+        for j in range(3):
+            head = (3 * s + j) % heads
+
+            @pl.when(h != head)
+            def _():
+                part = wall.at[s, :, pl.ds(HD * j, HD)]
+                await_copy(part, w2_send.at[3 * s + j])
+
+    out.finish()
+
+
+def front(tokens, w_qkv, kv_pool):
+    reqs, toks, width = tokens.shape
+    slots, page, _ = kv_pool.shape
+    owners, planes, heads = 16, 8, 8
+    dma = pltpu.SemaphoreType.DMA
+    hbm = pl.BlockSpec(memory_space=pl.ANY)
+    vmem = pl.BlockSpec(memory_space=pltpu.VMEM)
+    bf16 = jnp.bfloat16
+    return pl.pallas_call(
+        front_kernel,
+        out_shape=(
+            jax.ShapeDtypeStruct((2, owners * toks, HD), bf16),
+            jax.ShapeDtypeStruct((owners, toks, 2 * HD), bf16),
+            jax.ShapeDtypeStruct((heads * slots, page, 2 * HD), bf16),
+            jax.ShapeDtypeStruct((reqs, toks, 2 * heads * HD), bf16),
+        ),
+        in_specs=[hbm, hbm, hbm],
+        out_specs=(vmem, vmem, hbm, hbm),
+        scratch_shapes=[
+            pltpu.VMEM((owners, toks, width), bf16),
+            pltpu.VMEM((planes,) + w_qkv.shape, bf16),
+            pltpu.VMEM((owners, w_qkv.shape[0], 3 * HD), bf16),
+            dma((15,)),
+            dma((owners,)),
+            dma((planes - 1,)),
+            dma((planes,)),
+            dma((3 * planes,)),
+            dma((heads, 3)),
+            dma((heads,)),
+            dma((heads,)),
+            dma((heads, 2)),
+            dma((heads, 2)),
+            dma((owners, 2)),
+            dma((owners, 2)),
+            dma((2,)),
+            dma((6,)),
+        ],
+        compiler_params=pltpu.CompilerParams(
+            collective_id=0, has_side_effects=True, vmem_limit_bytes=40 << 20
+        ),
+        name="front",
+    )(tokens, w_qkv, kv_pool)
+
+
 def body(tokens, w_qkv, w_out, ln_gain, ln_bias, kv_pool, page_table, prefix_len, group_of):
     reqs, toks, width = tokens.shape
     owners = lax.axis_size("fsdp")
     heads = owners // 2
     inner = heads * HD
-    f = lax.axis_index("fsdp")
-    y = f // heads
     rows = toks * owners
-    rowsets = [list(range(heads)), list(range(heads, 2 * heads))]
     flip = [(i, (i + heads) % owners) for i in range(owners)]
 
-    wall = lax.all_gather(w_qkv, "dp", axis=1, tiled=True)
-    wh = wall.reshape(wall.shape[0], 3, heads, HD).transpose(2, 0, 1, 3)
-    wh = wh.reshape(1, heads, wall.shape[0], 3 * HD)
-    wh = jnp.concatenate([wh, wh], 0).reshape(owners, wall.shape[0], 3 * HD)
-    wh = lax.all_to_all(wh, "fsdp", 0, 0, tiled=True).reshape(width, 3 * HD)
-    sent = jnp.repeat(tokens, heads, axis=0)
-    mine = lax.all_to_all(sent, "fsdp", 0, 0, tiled=True).reshape(rows, width)
-    qkv = jnp.dot(mine, wh, preferred_element_type=jnp.float32).astype(jnp.bfloat16)
-    q, k, v = qkv[:, :HD], qkv[:, HD : 2 * HD], qkv[:, 2 * HD :]
-
-    kv = lax.all_to_all(
-        qkv[:, HD:].reshape(owners, toks, 2 * HD), "fsdp", 0, 0, tiled=True
-    )
-    new_cache = (
-        kv.reshape(2, heads, toks, 2, HD).transpose(0, 2, 3, 1, 4).reshape(2, toks, 2 * inner)
-    )
-    slots, page = kv_pool.shape[0], kv_pool.shape[1]
-    ps = kv_pool.reshape(slots, page, 2, heads, HD).transpose(3, 0, 1, 2, 4)
-    ps = lax.all_to_all(
-        ps.reshape(heads, slots, page, 2 * HD), "fsdp", 0, 0, axis_index_groups=rowsets, tiled=True
-    )
-    pool = ps.reshape(heads * slots, page, 2 * HD)
-    q_par = lax.ppermute(q, "fsdp", flip)
+    q2, kv, pool, new_cache = front(tokens, w_qkv, kv_pool)
+    kv = kv.reshape(rows, 2 * HD)
+    k, v = kv[:, :HD], kv[:, HD:]
     o1, s1, o2, s2 = attention(
-        page_table, prefix_len, group_of, jnp.stack([q, q_par]), k, v, pool
+        page_table, prefix_len, group_of, q2, k, v, pool
     )
     o2, s2 = lax.ppermute(o2, "fsdp", flip), lax.ppermute(s2, "fsdp", flip)
     top = jnp.maximum(s1[0], s2[0])

time: 266 us -> 177 us (0.67)
  Pallas kernels: 6.24 us -> 93.1 us
  waiting for transfers between devices: 96.8 us -> 13.2 us
  blocking collectives: 74.9 us -> 33.4 us
  starting transfers between devices: 45.9 us -> 11.7 us
  local copies, waits for them, and re-layouts: 15.4 us -> 5.39 us
  matrix products: 8 us -> 3 us
    pallas_call x0 -> x1, Pallas kernels: none -> 87.4 us  [front(): pl.pallas_call(front_kernel, out_shape=(jax.ShapeDtypeStruct((2, owners *...]
    all_to_all x4 -> x0, waiting for transfers between devices: 84.2 us -> none  [the longest x1 63.8 us: body(): mine = lax.all_to_all(sent, 'fsdp', 0, 0, tiled=True).reshape(rows, width)]
    all_to_all x4 -> x0, starting transfers between devices: 37.4 us -> none  [the longest x1 16.8 us: body(): mine = lax.all_to_all(sent, 'fsdp', 0, 0, tiled=True).reshape(rows, width)]
    all_gather x1 -> x0, blocking collectives: 33.7 us -> none  [body(): wall = lax.all_gather(w_qkv, 'dp', axis=1, tiled=True)]
    all_gather x1, blocking collectives: 41.2 us -> 33.4 us  [body(): lax.all_gather(w_out, 'dp', axis=1, tiled=True)]
    ppermute x1 -> x0, waiting for transfers between devices: 6.68 us -> none  [body(): q_par = lax.ppermute(q, 'fsdp', flip)]
    reshape x5 -> x0, local copies, waits for them, and re-layouts: 6.07 us -> none  [the longest x1 2.69 us: body(): ps.reshape(heads, slots, page, 2 * HD)]
    ppermute x2, waiting for transfers between devices: 0.39 us -> 5.96 us  [body(): o2, s2 = (lax.ppermute(o2, 'fsdp', flip), lax.ppermute(s2, 'fsdp', flip))]
  transfers between devices with their start and end apart: 9 -> 4, of which waited for: 6 -> 2; matrix products, arithmetic and copies ran while one was open for 6% -> 1% of each run, Pallas kernels for 2% -> 53%
where the time goes in v2:
time: 177 us; the launch traced here: 175 us
  Pallas kernels  93.1 us (53%)
  blocking collectives  33.4 us (19%)
  between operations  14.2 us (8%)
  waiting for transfers between devices  13.2 us (7%)
  starting transfers between devices  11.7 us (7%)
  local copies, waits for them, and re-layouts  5.39 us (3%)
  matrix products  3 us (2%)
    pallas_call x1, Pallas kernels, front(): pl.pallas_call(front_kernel, out_shape=(jax.ShapeDtypeStruct((2, owners *...  87.4 us
    all_gather x1, blocking collectives, body(): lax.all_gather(w_out, 'dp', axis=1, tiled=True)  33.4 us
    all_to_all x1, starting transfers between devices, body(): attn = lax.all_to_all(attn, 'fsdp', 0, 0, tiled=True)  10.1 us
    all_to_all x1, waiting for transfers between devices, body(): attn = lax.all_to_all(attn, 'fsdp', 0, 0, tiled=True)  7.2 us
    ppermute x2, waiting for transfers between devices, body(): o2, s2 = (lax.ppermute(o2, 'fsdp', flip), lax.ppermute(s2, 'fsdp', flip))  5.96 us
    pallas_call x1, Pallas kernels, attention(): pl.pallas_call(functools.partial(attention_kernel, slots), out_shape=(jax...  5.75 us
    unnamed x19, local copies, waits for them, and re-layouts  4.34 us
  transfers between devices with their start and end apart: 4, of which 2 were waited for; matrix products, arithmetic and copies ran while one was open for 1% of the time, Pallas kernels for 53%

profile of v2, /device:TPU:1, one launch (start us, length us, event | category | flops | bytes accessed | tf_op | source)
XLA Modules:
  0.0 175.4 jit_solution(4070558300739006848)
XLA Ops:
  7.2 0.0 copy-start.4
  7.2 0.0 copy-start.5
  7.2 0.0 copy-start.6
  7.2 0.0 all-gather.2.cloned.1.call-start
  7.2 33.4 %all_gather.6 = bf16[64,2048]{1,0:T(8,128)(2,1)} all-gather(bf16[64,256]{1,0:T(8,128)(2,1)} %param.11), channel_id=1, replica_groups=mesh['dp'=8,'fsdp'=16] {'dp'}, dimensions={1}, use_global_device_ids=true | all-gather | bytes 294912 | tf_op jit(solution)/shard_map/all_gather | solution.py:454
  40.6 0.0 all-gather.2.cloned.1.call-update
  40.7 0.0 copy-start
  40.7 1.6 copy-done
  42.3 0.0 copy-start.1
  42.3 1.0 copy-done.1
  43.3 0.0 copy-start.3
  43.3 0.9 copy-done.3
  44.2 0.0 copy-start.2
  44.2 87.4 %front.1 = (bf16[2,1024,128]{2,1,0:T(8,128)(2,1)S(1)}, bf16[16,64,256]{2,1,0:T(8,128)(2,1)S(1)}, bf16[32,128,256]{2,1,0:T(8,128)(2,1)S(1)}, bf16[2,64,2048]{2,1,0:T(8,128)(2,1)S(1)}) custom-call(bf16[2,64,2048]{2,1,0:T(8,128)(2,1)S(1)} %copy-done.1, bf16[128,384]{1,0:T(8,128)(2,1)S(1)} %copy-done.3, bf16[4,128,2048]{2,1,0:T(8,128)(2,1)S(1)} %copy-done), custom_call_target="tpu_custom_call" | custom-call | tf_op jit(solution)/shard_map/front/pallas_call | solution.py:395
  131.6 0.0 copy-done.4
  131.6 0.0 copy-done.5
  131.7 0.0 copy-done.6
  131.7 5.7 %attend.1 = (f32[128,1024]{1,0:T(8,128)S(1)}, f32[8,1024]{1,0:T(8,128)S(1)}, bf16[128,1024]{1,0:T(8,128)(2,1)S(1)}, f32[8,1024]{1,0:T(8,128)S(1)}) custom-call(s32[4,16]{1,0:T(4,128)S(1)} %copy-done.4, s32[4]{0:T(128)S(1)} %copy-done.5, s32[2]{0:T(128)S(1)} %copy-done.6, bf16[2,1024,128]{2,1,0:T(8,128)(2,1)S(1)} %get-tuple-element.10.q_ref, ...), custom_call_target="tpu_custom_call" | custom-call | tf_op jit(solution)/shard_map/attend/pallas_call | solution.py:131
  137.4 1.4 collective-permute-start.1
  138.8 0.1 collective-permute-start
  139.0 6.0 %collective-permute-done = f32[8,1024]{1,0:T(8,128)S(1)} collective-permute-done((f32[8,1024]{1,0:T(8,128)S(1)}, f32[8,1024]{1,0:T(8,128)S(1)}, u32[]{:S(2)}, u32[]{:S(2)}) %collective-permute-start) | collective-permute-done | bytes 32800 | tf_op jit(solution)/shard_map/ppermute | solution.py:445
  144.9 0.0 collective-permute-done.1
  145.0 0.1 fusion.2
  145.1 0.8 copy.11
  145.9 0.0 copy-start.7
  145.9 0.0 copy-start.8
  145.9 10.1 %all-to-all-start = ((bf16[16,64,128]{2,1,0:T(8,128)(2,1)}), bf16[16,64,128]{2,1,0:T(8,128)(2,1)S(1)}, u32[]{:S(2)}, u32[]{:S(2)}) async-start(bf16[16,64,128]{2,1,0:T(8,128)(2,1)} %bitcast.6), calls=%async_computation | async-start | bytes 524288 | tf_op jit(solution)/shard_map/all_to_all | solution.py:451
  156.0 7.2 %all-to-all-done = bf16[16,64,128]{2,1,0:T(8,128)(2,1)S(1)} async-done(((bf16[16,64,128]{2,1,0:T(8,128)(2,1)}), bf16[16,64,128]{2,1,0:T(8,128)(2,1)S(1)}, u32[]{:S(2)}, u32[]{:S(2)}) %all-to-all-start) | async-done | bytes 262176 | tf_op jit(solution)/shard_map/all_to_all | solution.py:451
  163.2 0.2 copy.12
  163.4 0.0 all-gather.2.cloned.1.call-done
  163.5 0.0 copy-done.2
  163.5 3.0 %fusion.9 = (f32[128]{0:T(128)S(1)}, f32[128,2048]{1,0:T(8,128)S(1)}) fusion(bf16[1024,2048]{1,0:T(8,128)(2,1)} %all-gather.2.cloned.1.call-done, bf16[16,8,8,128]{3,2,1,0:T(8,128)(2,1)S(1)} %bitcast.22, bf16[128,2048]{1,0:T(8,128)(2,1)S(1)} %bitcast.20), kind=kOutput, calls=%fused_computation.16 | convolution fusion | flops 537657216 | bytes 6029824 | tf_op jit(solution)/shard_map/dot_general | solution.py:455
  166.5 0.3 multiply_reduce_fusion
  166.7 0.0 copy-done.7
  166.8 0.0 copy-done.8
  166.8 1.0 add_convert_fusion
  167.8 0.8 copy.21
  (4 shorter events, 0.1 us)
Async XLA Ops:
  7.2 124.5 %copy-start.4 = (s32[4,16]{1,0:T(4,128)S(1)}, s32[4,16]{1,0:T(4,128)}, u32[]{:S(2)}) copy-start(s32[4,16]{1,0:T(4,128)} %page_table.1) | copy-start | bytes 772
  7.2 124.5 %copy-start.5 = (s32[4]{0:T(128)S(1)}, s32[4]{0:T(128)}, u32[]{:S(2)}) copy-start(s32[4]{0:T(128)} %prefix_len.1) | copy-start | bytes 52
  7.2 124.5 %copy-start.6 = (s32[2]{0:T(128)S(1)}, s32[2]{0:T(128)}, u32[]{:S(2)}) copy-start(s32[2]{0:T(128)} %group_of.1) | copy-start | bytes 28
  7.2 156.3 %all-gather.2.cloned.1.call-start = ((), (), s32[]{:S(2)}) async-start(), calls=%async_computation.1 | async-start | bytes 4456448 | tf_op jit(solution)/shard_map/all_gather | solution.py:454
  40.7 1.6 copy-start
  42.3 1.0 copy-start.1
  43.3 0.9 copy-start.3
  44.2 119.3 %copy-start.2 = (bf16[2,64,2048]{2,1,0:T(8,128)(2,1)S(1)}, bf16[2,64,2048]{2,1,0:T(8,128)(2,1)}, u32[]{:S(2)}) copy-start(bf16[2,64,2048]{2,1,0:T(8,128)(2,1)} %tokens.1) | copy-start | bytes 1572868
  137.4 7.5 %collective-permute-start.1 = (bf16[128,1024]{1,0:T(8,128)(2,1)S(1)}, bf16[128,1024]{1,0:T(8,128)(2,1)S(1)}, u32[]{:S(2)}, u32[]{:S(2)}) collective-permute-start(bf16[128,1024]{1,0:T(8,128)(2,1)S(1)} %get-tuple-element.16), channel_id=1, source_target_pairs={{0,8},{1,9},{2,10},{3,11},{4,12},{5,13},{6,14},{7,15},{8,0},{9,1},... | collective-permute-start | bytes 786440 | tf_op jit(solution)/shard_map/ppermute | solution.py:445
  138.8 6.1 %collective-permute-start = (f32[8,1024]{1,0:T(8,128)S(1)}, f32[8,1024]{1,0:T(8,128)S(1)}, u32[]{:S(2)}, u32[]{:S(2)}) collective-permute-start(f32[8,1024]{1,0:T(8,128)S(1)} %get-tuple-element.15), channel_id=1, source_target_pairs={{0,8},{1,9},{2,10},{3,11},{4,12},{5,13},{6,14},{7,15},{8,0},{9,1},... | collective-permute-start | bytes 98312 | tf_op jit(solution)/shard_map/ppermute | solution.py:445
  145.9 20.8 %copy-start.7 = (f32[2048]{0:T(1024)S(1)}, f32[2048]{0:T(1024)}, u32[]{:S(2)}) copy-start(f32[2048]{0:T(1024)} %param.13) | copy-start | bytes 24580
  145.9 20.8 %copy-start.8 = (f32[2048]{0:T(1024)S(1)}, f32[2048]{0:T(1024)}, u32[]{:S(2)}) copy-start(f32[2048]{0:T(1024)} %param.12) | copy-start | bytes 24580
  145.9 17.3 %all-to-all-start = ((bf16[16,64,128]{2,1,0:T(8,128)(2,1)}), bf16[16,64,128]{2,1,0:T(8,128)(2,1)S(1)}, u32[]{:S(2)}, u32[]{:S(2)}) async-start(bf16[16,64,128]{2,1,0:T(8,128)(2,1)} %bitcast.6), calls=%async_computation | async-start | bytes 524288 | tf_op jit(solution)/shard_map/all_to_all | solution.py:451
Sparse Core Ops, SparseCore 0:
  40.8 59.7 all-gather.1

commit v3 on v2

--- a/solution.py
+++ b/solution.py
@@ -183,11 +183,13 @@
 def front_kernel(
     tokens,
     w_ref,
+    wo_ref,
     pool_in,
     q2,
     kv,
     pool,
     cache,
+    wo,
     x_buf,
     wall,
     wh,
@@ -205,6 +207,10 @@
     c_recv,
     q_sem,
     local_sem,
+    o1_send,
+    o1_recv,
+    o2_send,
+    o2_recv,
 ):
     d = lax.axis_index("dp")
     f = lax.axis_index("fsdp")
@@ -231,11 +237,20 @@
         pl.semaphore_signal(
             barrier, inc=1, device_id={"dp": lax.rem(d + k, planes)}, device_id_type=MESH
         )
+    z, z_pair = d // 2, lax.rem(d, 2)
+    other_plane = 2 * z + 1 - z_pair
+    for k in range(1, owners):
+        pl.semaphore_signal(
+            barrier,
+            inc=1,
+            device_id={"dp": other_plane, "fsdp": lax.rem(f + k, owners)},
+            device_id_type=MESH,
+        )
     own_w = pltpu.make_async_copy(w_ref, wall.at[d], local_sem.at[0])
     own_w.start()
     own_x = pltpu.make_async_copy(tokens.at[y], x_buf.at[f], local_sem.at[1])
     own_x.start()
-    pl.semaphore_wait(barrier, owners + planes - 2)
+    pl.semaphore_wait(barrier, 2 * owners + planes - 3)
 
     out = Copies()
     for k in range(1, planes):
@@ -250,6 +265,33 @@
     send_x(1, tokens.at[y], f, right)
     send_x(2, tokens.at[y], f, left)
     send_x(3, tokens.at[y], f, twin)
+
+    group = f // heads
+    for p in range(2):
+        for k in range(heads):
+            dest = lax.rem(f // 2 + k, heads) * 2 + z_pair
+            plane = d if p == 0 else other_plane
+            sem = o1_send.at[p * heads + k]
+            dst = wo.at[d, f]
+            if p == 0 and k == 0:
+
+                @pl.when(core == z_pair)
+                def _():
+                    pltpu.make_async_copy(wo_ref, dst, o1_recv.at[group]).start()
+
+                @pl.when(core != z_pair)
+                def _():
+                    pltpu.make_async_remote_copy(
+                        src_ref=wo_ref,
+                        dst_ref=dst,
+                        send_sem=sem,
+                        recv_sem=o1_recv.at[group],
+                        device_id={"fsdp": dest},
+                        device_id_type=MESH,
+                    ).start()
+
+            else:
+                out.send(wo_ref, dst, sem, o1_recv.at[group], {"dp": plane, "fsdp": dest})
 
     for s in range(planes):
 
@@ -306,6 +348,28 @@
     send_x(11, x_buf.at[b_right], b_right, twin)
     await_copy(x_buf.at[b_left], x_recv.at[b_left])
     send_x(12, x_buf.at[b_left], b_left, twin)
+
+    def half(plane, n):
+        return wo.at[plane, pl.ds(n * heads, heads)]
+
+    def send_o(n, plane, part, dp, ff):
+        out.send(
+            half(plane, part),
+            half(plane, part),
+            o2_send.at[n],
+            o2_recv.at[plane, part],
+            {"dp": dp, "fsdp": ff},
+        )
+
+    def z_plane(k, c):
+        return 2 * lax.rem(z + k, 4) + c
+
+    up, down = z_plane(1, z_pair), z_plane(3, z_pair)
+    for part in range(2):
+        await_copy(half(z_plane(0, core), part), o1_recv.at[part])
+        send_o(3 * part, z_plane(0, core), part, up, f)
+        send_o(3 * part + 1, z_plane(0, core), part, down, f)
+        send_o(3 * part + 2, z_plane(0, core), part, d, twin)
 
     own_pool = []
     for k in range(heads):
@@ -323,6 +387,15 @@
                     src, dst, p_send.at[k, t], p_recv.at[h, t], {"fsdp": y * heads + head}
                 )
 
+    for n, (k, part) in enumerate(((3, 0), (1, 1), (1, 0), (3, 1))):
+        plane = z_plane(k, core)
+        await_copy(half(plane, part), o2_recv.at[plane, part])
+        if n == 0:
+            send_o(6, plane, part, up, f)
+        if n == 1:
+            send_o(7, plane, part, down, f)
+        send_o(8 + n, plane, part, d, twin)
+
     await_copy(x_buf.at[a_far], x_recv.at[a_far])
     send_x(13, x_buf.at[a_far], a_far, twin)
     await_copy(x_buf.at[b_far], x_recv.at[b_far])
@@ -357,6 +430,19 @@
                 own_cache.append(copy)
             else:
                 out.send(src, dst, c_send.at[k, t], c_recv.at[f, t], {"fsdp": who})
+
+    for part in range(2):
+        plane = z_plane(2, core)
+        await_copy(half(plane, part), o2_recv.at[plane, part])
+        send_o(12 + part, plane, part, d, twin)
+    for k in range(4):
+        for part in range(2):
+            plane = z_plane(k, 1 - core)
+            await_copy(half(plane, part), o2_recv.at[plane, part])
+
+    @pl.when(core != z_pair)
+    def _():
+        await_copy(wo.at[d, f], o1_send.at[0])
 
     await_copy(q2.at[1], q_sem.at[1])
     for copy in own_pool + own_cache:
@@ -384,7 +470,7 @@
     out.finish()
 
 
-def front(tokens, w_qkv, kv_pool):
+def front(tokens, w_qkv, w_out, kv_pool):
     reqs, toks, width = tokens.shape
     slots, page, _ = kv_pool.shape
     owners, planes, heads = 16, 8, 8
@@ -399,9 +485,10 @@
             jax.ShapeDtypeStruct((owners, toks, 2 * HD), bf16),
             jax.ShapeDtypeStruct((heads * slots, page, 2 * HD), bf16),
             jax.ShapeDtypeStruct((reqs, toks, 2 * heads * HD), bf16),
+            jax.ShapeDtypeStruct((planes, owners) + w_out.shape, bf16),
         ),
-        in_specs=[hbm, hbm, hbm],
-        out_specs=(vmem, vmem, hbm, hbm),
+        in_specs=[hbm, hbm, hbm, hbm],
+        out_specs=(vmem, vmem, hbm, hbm, hbm),
         scratch_shapes=[
             pltpu.VMEM((owners, toks, width), bf16),
             pltpu.VMEM((planes,) + w_qkv.shape, bf16),
@@ -420,44 +507,148 @@
             dma((owners, 2)),
             dma((2,)),
             dma((6,)),
+            dma((owners,)),
+            dma((2,)),
+            dma((15,)),
+            dma((planes, 2)),
         ],
         compiler_params=pltpu.CompilerParams(
             collective_id=0, has_side_effects=True, vmem_limit_bytes=40 << 20
         ),
         name="front",
-    )(tokens, w_qkv, kv_pool)
+    )(tokens, w_qkv, w_out, kv_pool)
+
+
+def tail_kernel(
+    tokens,
+    o1,
+    s1,
+    o2,
+    s2,
+    wo_hbm,
+    gain,
+    bias,
+    hidden,
+    o2_in,
+    s2_in,
+    at_out,
+    at_in,
+    wo,
+    mixed,
+    y_send,
+    y_recv,
+    a_send,
+    a_recv,
+    w_sem,
+):
+    f = lax.axis_index("fsdp")
+    owners = 16
+    heads = owners // 2
+    y, h = f // heads, lax.rem(f, heads)
+    across = (1 - y) * heads + h
+    planes, depth, cols = wo.shape
+    reqs, toks, width = tokens.shape
+    rows = owners * toks
+
+    barrier = pltpu.get_barrier_semaphore()
+    for k in range(1, owners):
+        pl.semaphore_signal(
+            barrier, inc=1, device_id={"fsdp": lax.rem(f + k, owners)}, device_id_type=MESH
+        )
+    loads = []
+    for p in range(planes):
+        load = pltpu.make_async_copy(wo_hbm.at[p], wo.at[p], w_sem.at[p])
+        load.start()
+        loads.append(load)
+    pl.semaphore_wait(barrier, owners - 1)
+    out = Copies()
+    out.send(s2, s2_in, y_send.at[0], y_recv.at[0], {"fsdp": across})
+    out.send(o2, o2_in, y_send.at[1], y_recv.at[1], {"fsdp": across})
+    await_copy(s2_in, y_recv.at[0])
+    top = jnp.maximum(s1[0:1, :], s2_in[0:1, :])
+    f1 = jnp.exp(s1[0:1, :] - top)
+    f2 = jnp.exp(s2_in[0:1, :] - top) * s2_in[1:2, :]
+    denom = s1[1:2, :] * f1 + f2
+    await_copy(o2_in, y_recv.at[1])
+    attn = (o1[...] * f1 + o2_in[...].astype(jnp.float32) * f2) / denom
+    at_out[...] = attn.T.astype(jnp.bfloat16).reshape(owners, toks, HD)
+    at_in[y, :, pl.ds(pl.multiple_of(h * HD, HD), HD)] = at_out[f]
+    for k in range(1, owners):
+        who = lax.rem(f + k, owners)
+        dst = at_in.at[y, :, pl.ds(pl.multiple_of(h * HD, HD), HD)]
+        out.send(at_out.at[who], dst, a_send.at[k], a_recv.at[f], {"fsdp": who})
+    for k in range(1, owners):
+        who = lax.rem(f + k, owners)
+        col = pl.multiple_of(lax.rem(who, heads) * HD, HD)
+        await_copy(at_in.at[who // heads, :, pl.ds(col, HD)], a_recv.at[who])
+    left_rows = at_in[...].reshape(reqs * toks, depth)
+    total = jnp.zeros((reqs * toks, 1), jnp.float32)
+    for p in range(planes):
+        loads[p].wait()
+        part = dot32(left_rows, wo[p], NN)
+        part = part + tokens[:, :, p * cols : (p + 1) * cols].reshape(
+            reqs * toks, cols
+        ).astype(jnp.float32)
+        total = total + jnp.sum(part, axis=1, keepdims=True)
+        mixed[:, p * cols : (p + 1) * cols] = part
+    mean = total * (1.0 / width)
+    square = jnp.zeros((reqs * toks, 1), jnp.float32)
+    for p in range(planes):
+        centred = mixed[:, p * cols : (p + 1) * cols] - mean
+        square = square + jnp.sum(centred * centred, axis=1, keepdims=True)
+    scale = lax.rsqrt(square * (1.0 / width) + LN_EPS)
+    for p in range(planes):
+        at = slice(p * cols, (p + 1) * cols)
+        normed = (mixed[:, at] - mean) * scale * gain[0:1, at] + bias[0:1, at]
+        hidden[:, :, at] = normed.astype(jnp.bfloat16).reshape(reqs, toks, cols)
+    out.finish()
+
+
+def tail(tokens, o1, s1, o2, s2, wo, gain, bias):
+    reqs, toks, width = tokens.shape
+    owners, planes = 16, 8
+    dma = pltpu.SemaphoreType.DMA
+    hbm = pl.BlockSpec(memory_space=pl.ANY)
+    vmem = pl.BlockSpec(memory_space=pltpu.VMEM)
+    bf16 = jnp.bfloat16
+    wo = wo.reshape(planes, HD * owners // 2, width // planes)
+    return pl.pallas_call(
+        tail_kernel,
+        out_shape=jax.ShapeDtypeStruct(tokens.shape, bf16),
+        in_specs=[vmem, vmem, vmem, vmem, vmem, hbm, vmem, vmem],
+        out_specs=vmem,
+        scratch_shapes=[
+            pltpu.VMEM(o2.shape, bf16),
+            pltpu.VMEM(s2.shape, jnp.float32),
+            pltpu.VMEM((owners, toks, HD), bf16),
+            pltpu.VMEM((reqs, toks, HD * owners // 2), bf16),
+            pltpu.VMEM(wo.shape, bf16),
+            pltpu.VMEM((reqs * toks, width), jnp.float32),
+            dma((2,)),
+            dma((2,)),
+            dma((owners,)),
+            dma((owners,)),
+            dma((planes,)),
+        ],
+        compiler_params=pltpu.CompilerParams(
+            collective_id=1, has_side_effects=True, vmem_limit_bytes=40 << 20
+        ),
+        name="tail",
+    )(tokens, o1, s1, o2, s2, wo, gain.reshape(1, width), bias.reshape(1, width))
 
 
 def body(tokens, w_qkv, w_out, ln_gain, ln_bias, kv_pool, page_table, prefix_len, group_of):
     reqs, toks, width = tokens.shape
     owners = lax.axis_size("fsdp")
-    heads = owners // 2
-    inner = heads * HD
     rows = toks * owners
-    flip = [(i, (i + heads) % owners) for i in range(owners)]
-
-    q2, kv, pool, new_cache = front(tokens, w_qkv, kv_pool)
+    q2, kv, pool, new_cache, wo = front(tokens, w_qkv, w_out, kv_pool)
     kv = kv.reshape(rows, 2 * HD)
     k, v = kv[:, :HD], kv[:, HD:]
     o1, s1, o2, s2 = attention(
         page_table, prefix_len, group_of, q2, k, v, pool
     )
-    o2, s2 = lax.ppermute(o2, "fsdp", flip), lax.ppermute(s2, "fsdp", flip)
-    top = jnp.maximum(s1[0], s2[0])
-    f1 = jnp.exp(s1[0] - top)
-    f2 = jnp.exp(s2[0] - top) * s2[1]
-    attn = (o1 * f1 + o2.astype(jnp.float32) * f2) / (s1[1] * f1 + f2)
-    attn = attn.T.astype(jnp.bfloat16).reshape(owners, toks, HD)
-    attn = lax.all_to_all(attn, "fsdp", 0, 0, tiled=True)
-    attn = attn.reshape(2, heads, toks, HD).transpose(0, 2, 1, 3).reshape(2 * toks, inner)
-
-    wo = lax.all_gather(lax.all_gather(w_out, "dp", axis=1, tiled=True), "fsdp", axis=0, tiled=True)
-    proj = jnp.dot(attn, wo, preferred_element_type=jnp.float32)
-    mixed = tokens.reshape(reqs * toks, width).astype(jnp.float32) + proj
-    centred = mixed - jnp.mean(mixed, axis=1, keepdims=True)
-    var = jnp.mean(centred * centred, axis=1, keepdims=True)
-    normed = centred * lax.rsqrt(var + LN_EPS) * ln_gain[None, :] + ln_bias[None, :]
-    return normed.astype(jnp.bfloat16).reshape(reqs, toks, width), new_cache
+    hidden = tail(tokens, o1, s1, o2, s2, wo, ln_gain, ln_bias)
+    return hidden, new_cache
 
 
 def solution(mesh):

time: 177 us -> 109 us (0.62)
  blocking collectives: 33.4 us -> 0 us
  between operations: 14.2 us -> 0.77 us
  waiting for transfers between devices: 13.2 us -> 0 us
  starting transfers between devices: 11.7 us -> 0 us
  Pallas kernels: 93.1 us -> 102 us
  matrix products: 3 us -> 0 us
    all_gather x1 -> x0, blocking collectives: 33.4 us -> none  [body(): lax.all_gather(w_out, 'dp', axis=1, tiled=True)]
    pallas_call x0 -> x1, Pallas kernels: none -> 22.5 us  [tail(): pl.pallas_call(tail_kernel, out_shape=jax.ShapeDtypeStruct(tokens.shape,...]
    pallas_call x1, Pallas kernels: 87.4 us -> 72.8 us  [front(): pl.pallas_call(front_kernel, out_shape=(jax.ShapeDtypeStruct((2, owners *...]
    all_to_all x1 -> x0, starting transfers between devices: 10.1 us -> none  [body(): attn = lax.all_to_all(attn, 'fsdp', 0, 0, tiled=True)]
    all_to_all x1 -> x0, waiting for transfers between devices: 7.2 us -> none  [body(): attn = lax.all_to_all(attn, 'fsdp', 0, 0, tiled=True)]
    ppermute x2 -> x0, waiting for transfers between devices: 5.96 us -> none  [body(): o2, s2 = (lax.ppermute(o2, 'fsdp', flip), lax.ppermute(s2, 'fsdp', flip))]
    dot_general x1 -> x0, matrix products: 3 us -> none  [body(): proj = jnp.dot(attn, wo, preferred_element_type=jnp.float32)]
    unnamed x19 -> x22, local copies, waits for them, and re-layouts: 4.34 us -> 5.91 us
  transfers between devices with their start and end apart: 4 -> 0, of which waited for: 2 -> 0; matrix products, arithmetic and copies ran while one was open for 1% -> 0% of each run, Pallas kernels for 53% -> 0%
where the time goes in v3:
time: 109 us
  Pallas kernels  102 us (94%)
  local copies, waits for them, and re-layouts  5.95 us (5%)
    pallas_call x1, Pallas kernels, front(): pl.pallas_call(front_kernel, out_shape=(jax.ShapeDtypeStruct((2, owners *...  72.8 us
    pallas_call x1, Pallas kernels, tail(): pl.pallas_call(tail_kernel, out_shape=jax.ShapeDtypeStruct(tokens.shape,...  22.5 us
    pallas_call x1, Pallas kernels, attention(): pl.pallas_call(functools.partial(attention_kernel, slots), out_shape=(jax...  6.73 us
    unnamed x22, local copies, waits for them, and re-layouts  5.91 us

profile of v3, /device:TPU:1, one launch (start us, length us, event | category | flops | bytes accessed | tf_op | source)
XLA Modules:
  0.0 108.7 jit_solution(7530572113539383895)
XLA Ops:
  0.6 0.0 copy-start.9
  0.6 0.0 copy-start.8
  0.7 0.0 copy-start.7
  0.7 0.0 copy-start
  0.7 1.6 %copy-done = bf16[4,128,2048]{2,1,0:T(8,128)(2,1)S(1)} copy-done((bf16[4,128,2048]{2,1,0:T(8,128)(2,1)S(1)}, bf16[4,128,2048]{2,1,0:T(8,128)(2,1)}, u32[]{:S(2)}) %copy-start) | copy-done | bytes 2097176
  2.3 0.0 copy-start.1
  2.3 1.0 copy-done.1
  3.3 0.0 copy-start.3
  3.3 0.9 copy-done.3
  4.2 0.0 copy-start.4
  4.2 0.8 copy-done.4
  5.0 72.8 %front.1 = (bf16[2,1024,128]{2,1,0:T(8,128)(2,1)S(1)}, bf16[16,64,256]{2,1,0:T(8,128)(2,1)S(1)}, bf16[32,128,256]{2,1,0:T(8,128)(2,1)S(1)}, bf16[2,64,2048]{2,1,0:T(8,128)(2,1)S(1)}, bf16[8,16,64,256]{3,2,1,0:T(8,128)(2,1)S(1)}) custom-call(bf16[2,64,2048]{2,1,0:T(8,128)(2,1)S(1)} %copy-done.1, bf16[128,384]{1,0:T(8,128)(2,1)S(1)} %copy-done.3, ...), custom_call_target="tpu_custom_call" | custom-call | tf_op jit(solution)/shard_map/front/pallas_call | solution.py:481
  77.7 0.0 copy-start.2
  77.8 0.0 copy-start.5
  77.8 0.0 copy-start.6
  77.8 0.0 copy-done.9
  77.8 0.0 copy-done.8
  77.8 0.0 copy-done.7
  77.9 6.7 %attend.1 = (f32[128,1024]{1,0:T(8,128)S(1)}, f32[8,1024]{1,0:T(8,128)S(1)}, bf16[128,1024]{1,0:T(8,128)(2,1)S(1)}, f32[8,1024]{1,0:T(8,128)S(1)}) custom-call(s32[4,16]{1,0:T(4,128)S(1)} %copy-done.7, s32[4]{0:T(128)S(1)} %copy-done.8, s32[2]{0:T(128)S(1)} %copy-done.9, bf16[2,1024,128]{2,1,0:T(8,128)(2,1)S(1)} %get-tuple-element.11.q_ref, ...), custom_call_target="tpu_custom_call" | custom-call | tf_op jit(solution)/shard_map/attend/pallas_call | solution.py:131
  84.6 0.0 copy-done.2
  84.6 0.0 copy-done.5
  84.6 0.0 copy-done.6
  84.6 22.5 %tail.1 = bf16[2,64,2048]{2,1,0:T(8,128)(2,1)S(1)} custom-call(bf16[2,64,2048]{2,1,0:T(8,128)(2,1)S(1)} %copy-done.2, f32[128,1024]{1,0:T(8,128)S(1)} %get-tuple-element.14.o1, f32[8,1024]{1,0:T(8,128)S(1)} %get-tuple-element.15.s1, bf16[128,1024]{1,0:T(8,128)(2,1)S(1)} %get-tuple-element.16.o2, f32[8,1024]{1,0:T(8,128)S(1)} %get-tuple-element.17.s2, ...), custom_call_target="tpu_custom_call" | custom-call | tf_op jit(solution)/shard_map/tail/pallas_call | solution.py:615
  107.1 0.8 copy.13
  107.9 0.8 copy.14
  (1 shorter events, 0.0 us)
Async XLA Ops:
  0.6 77.2 %copy-start.9 = (s32[2]{0:T(128)S(1)}, s32[2]{0:T(128)}, u32[]{:S(2)}) copy-start(s32[2]{0:T(128)} %group_of.1) | copy-start | bytes 28
  0.6 77.2 %copy-start.8 = (s32[4]{0:T(128)S(1)}, s32[4]{0:T(128)}, u32[]{:S(2)}) copy-start(s32[4]{0:T(128)} %prefix_len.1) | copy-start | bytes 52
  0.7 77.2 %copy-start.7 = (s32[4,16]{1,0:T(4,128)S(1)}, s32[4,16]{1,0:T(4,128)}, u32[]{:S(2)}) copy-start(s32[4,16]{1,0:T(4,128)} %page_table.1) | copy-start | bytes 772
  0.7 1.6 %copy-start = (bf16[4,128,2048]{2,1,0:T(8,128)(2,1)S(1)}, bf16[4,128,2048]{2,1,0:T(8,128)(2,1)}, u32[]{:S(2)}) copy-start(bf16[4,128,2048]{2,1,0:T(8,128)(2,1)} %pool_in.1) | copy-start | bytes 6291460
  2.3 1.0 copy-start.1
  3.3 0.9 copy-start.3
  4.2 0.8 copy-start.4
  77.7 6.9 %copy-start.2 = (bf16[2,64,2048]{2,1,0:T(8,128)(2,1)S(1)}, bf16[2,64,2048]{2,1,0:T(8,128)(2,1)}, u32[]{:S(2)}) copy-start(bf16[2,64,2048]{2,1,0:T(8,128)(2,1)} %tokens.3) | copy-start | bytes 1572868
  77.8 6.9 %copy-start.5 = (f32[2048]{0:T(1024)S(1)}, f32[2048]{0:T(1024)}, u32[]{:S(2)}) copy-start(f32[2048]{0:T(1024)} %param.12) | copy-start | bytes 24580
  77.8 6.8 %copy-start.6 = (f32[2048]{0:T(1024)S(1)}, f32[2048]{0:T(1024)}, u32[]{:S(2)}) copy-start(f32[2048]{0:T(1024)} %param.13) | copy-start | bytes 24580

commit v4 on v3

--- a/solution.py
+++ b/solution.py
@@ -50,7 +50,8 @@
     slot_list,
     base_list,
 ):
-    y = lax.axis_index("fsdp") // 8
+    f = lax.axis_index("fsdp")
+    y, x = f // 8, lax.rem(f, 8) // 2
     rows = q_ref.shape[1]
     page = pool_ref.shape[1]
     n_pages = page_table.shape[1]
@@ -67,7 +68,7 @@
 
             @pl.when(live)
             def _():
-                slot_list[count] = loc
+                slot_list[count] = lax.rem(loc, 4) * 8 + lax.rem(loc // 4 + 8 - 2 * x, 8)
                 base_list[count] = p * page
 
             return count + live.astype(jnp.int32)
@@ -203,6 +204,8 @@
     w3_recv,
     p_send,
     p_recv,
+    pz_send,
+    pz_recv,
     c_send,
     c_recv,
     q_sem,
@@ -246,7 +249,8 @@
             device_id={"dp": other_plane, "fsdp": lax.rem(f + k, owners)},
             device_id_type=MESH,
         )
-    own_w = pltpu.make_async_copy(w_ref, wall.at[d], local_sem.at[0])
+    wq = w_ref.shape[0] // 4
+    own_w = pltpu.make_async_copy(w_ref.at[pl.ds(wq * z, wq)], wall.at[d], local_sem.at[0])
     own_w.start()
     own_x = pltpu.make_async_copy(tokens.at[y], x_buf.at[f], local_sem.at[1])
     own_x.start()
@@ -254,9 +258,9 @@
 
     out = Copies()
     for k in range(1, planes):
-        out.send(
-            w_ref, wall.at[d], w1_send.at[k - 1], w1_recv.at[d], {"dp": lax.rem(d + k, planes)}
-        )
+        dest = lax.rem(d + k, planes)
+        src = w_ref.at[pl.ds(pl.multiple_of(wq * (dest // 2), wq), wq)]
+        out.send(src, wall.at[d], w1_send.at[k - 1], w1_recv.at[d], {"dp": dest})
 
     def send_x(n, src, who, dest):
         out.send(src, x_buf.at[who], x_send.at[n], x_recv.at[who], {"fsdp": dest})
@@ -266,33 +270,6 @@
     send_x(2, tokens.at[y], f, left)
     send_x(3, tokens.at[y], f, twin)
 
-    group = f // heads
-    for p in range(2):
-        for k in range(heads):
-            dest = lax.rem(f // 2 + k, heads) * 2 + z_pair
-            plane = d if p == 0 else other_plane
-            sem = o1_send.at[p * heads + k]
-            dst = wo.at[d, f]
-            if p == 0 and k == 0:
-
-                @pl.when(core == z_pair)
-                def _():
-                    pltpu.make_async_copy(wo_ref, dst, o1_recv.at[group]).start()
-
-                @pl.when(core != z_pair)
-                def _():
-                    pltpu.make_async_remote_copy(
-                        src_ref=wo_ref,
-                        dst_ref=dst,
-                        send_sem=sem,
-                        recv_sem=o1_recv.at[group],
-                        device_id={"fsdp": dest},
-                        device_id_type=MESH,
-                    ).start()
-
-            else:
-                out.send(wo_ref, dst, sem, o1_recv.at[group], {"dp": plane, "fsdp": dest})
-
     for s in range(planes):
 
         @pl.when(d == s)
@@ -306,7 +283,7 @@
         for j in range(3):
             t, head = divmod(3 * s + j, heads)
             src = wall.at[s, :, pl.ds(HD * j, HD)]
-            dst = wh.at[f, :, pl.ds(HD * t, HD)]
+            dst = wh.at[f, z, :, pl.ds(HD * t, HD)]
 
             @pl.when(h == head)
             def _():
@@ -322,6 +299,68 @@
                     device_id={"fsdp": y * heads + head},
                     device_id_type=MESH,
                 ).start()
+
+    up = lax.rem(d + 2, planes)
+    down = lax.rem(d + planes - 2, planes)
+
+    def z_at(k):
+        return lax.rem(z + k, 4)
+
+    def wh_part(n, zz):
+        row = y if n == 0 else 1 - y
+        return wh.at[pl.ds(row * heads, heads), zz]
+
+    def send_w(n, part, zz, dest):
+        src = wh_part(part, zz)
+        out.send(src, src, w3_send.at[n], w3_recv.at[zz, part], dest)
+
+    for r in range(heads):
+        for t in range(3):
+            await_copy(wh.at[y * heads + r, z, :, pl.ds(HD * t, HD)], w2_recv.at[r, t])
+    own_part = wh_part(0, z)
+    out.send(own_part, own_part, w3_send.at[0], w3_recv.at[z, 1], {"fsdp": across})
+    send_w(1, 0, z, {"dp": up})
+    send_w(2, 0, z, {"dp": down})
+
+    def pool_cols(t, head):
+        return pl.ds(pl.multiple_of((t * heads + head) * HD, HD), HD)
+
+    own_pool = []
+
+    def send_pool():
+        for t in range(2):
+            cols = pl.ds(t * HD, HD)
+            copy = pltpu.make_async_copy(
+                pool_in.at[:, :, pool_cols(t, h)], pool.at[:, core, :, cols], local_sem.at[2 + t]
+            )
+            copy.start()
+            own_pool.append(copy)
+            out.send(
+                pool_in.at[:, :, pool_cols(t, 2 * x + 1 - core)],
+                pool.at[:, core, :, cols],
+                p_send.at[0, t],
+                p_recv.at[0, t],
+                {"fsdp": twin},
+            )
+        for k in range(1, 4):
+            for c in range(2):
+                dest = at(y, x + k, c)
+                place = 2 * (4 - k) + core
+                for t in range(2):
+                    out.send(
+                        pool_in.at[z, :, pool_cols(t, lax.rem(dest, heads))],
+                        pool.at[z, place, :, pl.ds(t * HD, HD)],
+                        p_send.at[2 * k + c, t],
+                        p_recv.at[place, t],
+                        {"fsdp": dest},
+                    )
+
+    def pool_part(n, zz):
+        return pool.at[zz, pl.ds(2 + 3 * n, 3)]
+
+    def send_p(n, part, zz, dest):
+        src = pool_part(part, zz)
+        out.send(src, src, pz_send.at[n], pz_recv.at[zz, part], {"dp": dest})
 
     await_copy(x_buf.at[across], x_recv.at[across])
     send_x(4, x_buf.at[across], across, right)
@@ -336,12 +375,13 @@
     await_copy(x_buf.at[a_right], x_recv.at[a_right])
     send_x(9, x_buf.at[a_right], a_right, twin)
 
-    for r in range(heads):
-        src = y * heads + r
-        for t in range(3):
-            part = wh.at[src, :, pl.ds(HD * t, HD)]
-            await_copy(part, w2_recv.at[r, t])
-        out.send(wh.at[src], wh.at[src], w3_send.at[r], w3_recv.at[r], {"fsdp": across})
+    await_copy(wh_part(1, z), w3_recv.at[z, 1])
+    send_w(3, 1, z, {"dp": up})
+    send_w(4, 1, z, {"dp": down})
+    await_copy(wh_part(0, z_at(3)), w3_recv.at[z_at(3), 0])
+    send_w(5, 0, z_at(3), {"dp": up})
+
+    send_pool()
 
     await_copy(x_buf.at[b_right], x_recv.at[b_right])
     send_x(10, x_buf.at[b_right], b_right, left)
@@ -349,52 +389,42 @@
     await_copy(x_buf.at[b_left], x_recv.at[b_left])
     send_x(12, x_buf.at[b_left], b_left, twin)
 
-    def half(plane, n):
-        return wo.at[plane, pl.ds(n * heads, heads)]
-
-    def send_o(n, plane, part, dp, ff):
-        out.send(
-            half(plane, part),
-            half(plane, part),
-            o2_send.at[n],
-            o2_recv.at[plane, part],
-            {"dp": dp, "fsdp": ff},
-        )
-
-    def z_plane(k, c):
-        return 2 * lax.rem(z + k, 4) + c
-
-    up, down = z_plane(1, z_pair), z_plane(3, z_pair)
+    await_copy(wh_part(1, z_at(1)), w3_recv.at[z_at(1), 1])
+    send_w(6, 1, z_at(1), {"dp": down})
+
+    group = f // heads
+    for p in range(2):
+        for k in range(heads):
+            dest = lax.rem(f // 2 + k, heads) * 2 + z_pair
+            plane = d if p == 0 else other_plane
+            sem = o1_send.at[p * heads + k]
+            dst = wo.at[d, f]
+            if p == 0 and k == 0:
+
+                @pl.when(core == z_pair)
+                def _():
+                    pltpu.make_async_copy(wo_ref, dst, o1_recv.at[group]).start()
+
+                @pl.when(core != z_pair)
+                def _():
+                    pltpu.make_async_remote_copy(
+                        src_ref=wo_ref,
+                        dst_ref=dst,
+                        send_sem=sem,
+                        recv_sem=o1_recv.at[group],
+                        device_id={"fsdp": dest},
+                        device_id_type=MESH,
+                    ).start()
+
+            else:
+                out.send(wo_ref, dst, sem, o1_recv.at[group], {"dp": plane, "fsdp": dest})
+
+    for place in range(2, 8):
+        for t in range(2):
+            await_copy(pool.at[z, place, :, pl.ds(t * HD, HD)], p_recv.at[place, t])
     for part in range(2):
-        await_copy(half(z_plane(0, core), part), o1_recv.at[part])
-        send_o(3 * part, z_plane(0, core), part, up, f)
-        send_o(3 * part + 1, z_plane(0, core), part, down, f)
-        send_o(3 * part + 2, z_plane(0, core), part, d, twin)
-
-    own_pool = []
-    for k in range(heads):
-        head = lax.rem(h + k, heads)
-        for t in range(2):
-            cols = pl.ds(pl.multiple_of((t * heads + head) * HD, HD), HD)
-            src = pool_in.at[:, :, cols]
-            dst = pool.at[pl.ds(h * slots, slots), :, pl.ds(t * HD, HD)]
-            if k == 0:
-                copy = pltpu.make_async_copy(src, dst, local_sem.at[2 + t])
-                copy.start()
-                own_pool.append(copy)
-            else:
-                out.send(
-                    src, dst, p_send.at[k, t], p_recv.at[h, t], {"fsdp": y * heads + head}
-                )
-
-    for n, (k, part) in enumerate(((3, 0), (1, 1), (1, 0), (3, 1))):
-        plane = z_plane(k, core)
-        await_copy(half(plane, part), o2_recv.at[plane, part])
-        if n == 0:
-            send_o(6, plane, part, up, f)
-        if n == 1:
-            send_o(7, plane, part, down, f)
-        send_o(8 + n, plane, part, d, twin)
+        send_p(2 * part, part, z, up)
+        send_p(2 * part + 1, part, z, down)
 
     await_copy(x_buf.at[a_far], x_recv.at[a_far])
     send_x(13, x_buf.at[a_far], a_far, twin)
@@ -405,9 +435,8 @@
             who = at(yy, xx, 1 - core)
             await_copy(x_buf.at[who], x_recv.at[who])
     own_x.wait()
-    for r in range(heads):
-        src = (1 - y) * heads + r
-        await_copy(wh.at[src], w3_recv.at[r])
+    for k, part in ((1, 0), (3, 1), (2, 0), (2, 1)):
+        await_copy(wh_part(part, z_at(k)), w3_recv.at[z_at(k), part])
 
     @pl.loop(0, owners // 4)
     def _(i):
@@ -431,6 +460,40 @@
             else:
                 out.send(src, dst, c_send.at[k, t], c_recv.at[f, t], {"fsdp": who})
 
+    await_copy(pool_part(0, z_at(3)), pz_recv.at[z_at(3), 0])
+    send_p(4, 0, z_at(3), up)
+    await_copy(pool_part(1, z_at(1)), pz_recv.at[z_at(1), 1])
+    send_p(5, 1, z_at(1), down)
+
+    def half(plane, n):
+        return wo.at[plane, pl.ds(n * heads, heads)]
+
+    def send_o(n, plane, part, dp, ff):
+        out.send(
+            half(plane, part),
+            half(plane, part),
+            o2_send.at[n],
+            o2_recv.at[plane, part],
+            {"dp": dp, "fsdp": ff},
+        )
+
+    def z_plane(k, c):
+        return 2 * z_at(k) + c
+
+    for part in range(2):
+        plane = z_plane(0, core)
+        await_copy(half(plane, part), o1_recv.at[part])
+        send_o(3 * part, plane, part, up, f)
+        send_o(3 * part + 1, plane, part, down, f)
+        send_o(3 * part + 2, plane, part, d, twin)
+    for n, (k, part) in enumerate(((3, 0), (1, 1), (1, 0), (3, 1))):
+        plane = z_plane(k, core)
+        await_copy(half(plane, part), o2_recv.at[plane, part])
+        if n == 0:
+            send_o(6, plane, part, up, f)
+        if n == 1:
+            send_o(7, plane, part, down, f)
+        send_o(8 + n, plane, part, d, twin)
     for part in range(2):
         plane = z_plane(2, core)
         await_copy(half(plane, part), o2_recv.at[plane, part])
@@ -447,12 +510,10 @@
     await_copy(q2.at[1], q_sem.at[1])
     for copy in own_pool + own_cache:
         copy.wait()
-    for k in range(1, heads):
-        who = lax.rem(h + k, heads)
-        for t in range(2):
-            await_copy(
-                pool.at[pl.ds(who * slots, slots), :, pl.ds(t * HD, HD)], p_recv.at[who, t]
-            )
+    for t in range(2):
+        await_copy(pool.at[:, 1 - core, :, pl.ds(t * HD, HD)], p_recv.at[0, t])
+    for k, part in ((1, 0), (3, 1), (2, 0), (2, 1)):
+        await_copy(pool_part(part, z_at(k)), pz_recv.at[z_at(k), part])
     for k in range(1, owners):
         who = lax.rem(f + k, owners)
         for t in range(2):
@@ -475,7 +536,7 @@
     slots, page, _ = kv_pool.shape
     owners, planes, heads = 16, 8, 8
     dma = pltpu.SemaphoreType.DMA
-    hbm = pl.BlockSpec(memory_space=pl.ANY)
+    hbm = pl.BlockSpec(memory_space=pltpu.HBM)
     vmem = pl.BlockSpec(memory_space=pltpu.VMEM)
     bf16 = jnp.bfloat16
     return pl.pallas_call(
@@ -483,7 +544,7 @@
         out_shape=(
             jax.ShapeDtypeStruct((2, owners * toks, HD), bf16),
             jax.ShapeDtypeStruct((owners, toks, 2 * HD), bf16),
-            jax.ShapeDtypeStruct((heads * slots, page, 2 * HD), bf16),
+            jax.ShapeDtypeStruct((slots, heads, page, 2 * HD), bf16),
             jax.ShapeDtypeStruct((reqs, toks, 2 * heads * HD), bf16),
             jax.ShapeDtypeStruct((planes, owners) + w_out.shape, bf16),
         ),
@@ -491,18 +552,20 @@
         out_specs=(vmem, vmem, hbm, hbm, hbm),
         scratch_shapes=[
             pltpu.VMEM((owners, toks, width), bf16),
-            pltpu.VMEM((planes,) + w_qkv.shape, bf16),
-            pltpu.VMEM((owners, w_qkv.shape[0], 3 * HD), bf16),
+            pltpu.VMEM((planes, w_qkv.shape[0] // 4, w_qkv.shape[1]), bf16),
+            pltpu.VMEM((owners, 4, w_qkv.shape[0] // 4, 3 * HD), bf16),
             dma((15,)),
             dma((owners,)),
             dma((planes - 1,)),
             dma((planes,)),
             dma((3 * planes,)),
             dma((heads, 3)),
-            dma((heads,)),
-            dma((heads,)),
+            dma((7,)),
+            dma((4, 2)),
             dma((heads, 2)),
             dma((heads, 2)),
+            dma((6,)),
+            dma((4, 2)),
             dma((owners, 2)),
             dma((owners, 2)),
             dma((2,)),
@@ -608,7 +671,7 @@
     reqs, toks, width = tokens.shape
     owners, planes = 16, 8
     dma = pltpu.SemaphoreType.DMA
-    hbm = pl.BlockSpec(memory_space=pl.ANY)
+    hbm = pl.BlockSpec(memory_space=pltpu.HBM)
     vmem = pl.BlockSpec(memory_space=pltpu.VMEM)
     bf16 = jnp.bfloat16
     wo = wo.reshape(planes, HD * owners // 2, width // planes)
@@ -642,6 +705,7 @@
     owners = lax.axis_size("fsdp")
     rows = toks * owners
     q2, kv, pool, new_cache, wo = front(tokens, w_qkv, w_out, kv_pool)
+    pool = pool.reshape((-1,) + pool.shape[2:])
     kv = kv.reshape(rows, 2 * HD)
     k, v = kv[:, :HD], kv[:, HD:]
     o1, s1, o2, s2 = attention(

time: 109 us -> 112 us (1.028)
  Pallas kernels: 102 us -> 105 us
    pallas_call x1, Pallas kernels: 72.8 us -> 78.5 us  [front(): pl.pallas_call(front_kernel, out_shape=(jax.ShapeDtypeStruct((2, owners *...]
    pallas_call x1, Pallas kernels: 22.5 us -> 18.9 us  [tail(): pl.pallas_call(tail_kernel, out_shape=jax.ShapeDtypeStruct(tokens.shape,...]
where the time goes in v4:
time: 112 us; the launch traced here: 111 us
  Pallas kernels  105 us (94%)
  local copies, waits for them, and re-layouts  5.95 us (5%)
    pallas_call x1, Pallas kernels, front(): pl.pallas_call(front_kernel, out_shape=(jax.ShapeDtypeStruct((2, owners *...  78.5 us
    pallas_call x1, Pallas kernels, tail(): pl.pallas_call(tail_kernel, out_shape=jax.ShapeDtypeStruct(tokens.shape,...  18.9 us
    pallas_call x1, Pallas kernels, attention(): pl.pallas_call(functools.partial(attention_kernel, slots), out_shape=(jax...  7.34 us
    unnamed x22, local copies, waits for them, and re-layouts  5.91 us

profile of v4, /device:TPU:1, one launch (start us, length us, event | category | flops | bytes accessed | tf_op | source)
XLA Modules:
  0.0 111.5 jit_solution(208151198361146688)
XLA Ops:
  0.6 0.0 copy-start.9
  0.6 0.0 copy-start.8
  0.7 0.0 copy-start.7
  0.7 0.0 copy-start
  0.7 1.6 %copy-done = bf16[4,128,2048]{2,1,0:T(8,128)(2,1)S(1)} copy-done((bf16[4,128,2048]{2,1,0:T(8,128)(2,1)S(1)}, bf16[4,128,2048]{2,1,0:T(8,128)(2,1)}, u32[]{:S(2)}) %copy-start) | copy-done | bytes 2097176
  2.3 0.0 copy-start.1
  2.3 1.0 copy-done.1
  3.3 0.0 copy-start.3
  3.3 0.9 copy-done.3
  4.2 0.0 copy-start.4
  4.2 0.8 copy-done.4
  5.0 78.5 %front.1 = (bf16[2,1024,128]{2,1,0:T(8,128)(2,1)S(1)}, bf16[16,64,256]{2,1,0:T(8,128)(2,1)S(1)}, bf16[4,8,128,256]{3,2,1,0:T(8,128)(2,1)S(1)}, bf16[2,64,2048]{2...) custom-call(bf16[2,64,2048]{2,1,0:T(8,128)(2,1)S(1)} %copy-done.1, bf16[128,384]{1,0:T(8,128)(2,1)S(1)} %copy-done.3, ...), custom_call_target="tpu_custom_call" | custom-call | tf_op jit(solution)/shard_map/front/pallas_call | solution.py:542
  83.5 0.0 copy-start.2
  83.5 0.0 copy-start.5
  83.5 0.0 copy-start.6
  83.6 0.0 copy-done.9
  83.6 0.0 copy-done.8
  83.6 0.0 copy-done.7
  83.6 7.3 %attend.1 = (f32[128,1024]{1,0:T(8,128)S(1)}, f32[8,1024]{1,0:T(8,128)S(1)}, bf16[128,1024]{1,0:T(8,128)(2,1)S(1)}, f32[8,1024]{1,0:T(8,128)S(1)}) custom-call(s32[4,16]{1,0:T(4,128)S(1)} %copy-done.7, s32[4]{0:T(128)S(1)} %copy-done.8, s32[2]{0:T(128)S(1)} %copy-done.9, bf16[2,1024,128]{2,1,0:T(8,128)(2,1)S(1)} %get-tuple-element.11.q_ref, ...), custom_call_target="tpu_custom_call" | custom-call | tf_op jit(solution)/shard_map/attend/pallas_call | solution.py:132
  91.0 0.0 copy-done.2
  91.0 0.0 copy-done.5
  91.0 0.0 copy-done.6
  91.0 18.9 %tail.1 = bf16[2,64,2048]{2,1,0:T(8,128)(2,1)S(1)} custom-call(bf16[2,64,2048]{2,1,0:T(8,128)(2,1)S(1)} %copy-done.2, f32[128,1024]{1,0:T(8,128)S(1)} %get-tuple-element.14.o1, f32[8,1024]{1,0:T(8,128)S(1)} %get-tuple-element.15.s1, bf16[128,1024]{1,0:T(8,128)(2,1)S(1)} %get-tuple-element.16.o2, f32[8,1024]{1,0:T(8,128)S(1)} %get-tuple-element.17.s2, ...), custom_call_target="tpu_custom_call" | custom-call | tf_op jit(solution)/shard_map/tail/pallas_call | solution.py:678
  109.9 0.8 copy.13
  110.7 0.8 copy.14
  (1 shorter events, 0.0 us)
Async XLA Ops:
  0.6 83.0 %copy-start.9 = (s32[2]{0:T(128)S(1)}, s32[2]{0:T(128)}, u32[]{:S(2)}) copy-start(s32[2]{0:T(128)} %group_of.1) | copy-start | bytes 28
  0.6 83.0 %copy-start.8 = (s32[4]{0:T(128)S(1)}, s32[4]{0:T(128)}, u32[]{:S(2)}) copy-start(s32[4]{0:T(128)} %prefix_len.1) | copy-start | bytes 52
  0.7 83.0 %copy-start.7 = (s32[4,16]{1,0:T(4,128)S(1)}, s32[4,16]{1,0:T(4,128)}, u32[]{:S(2)}) copy-start(s32[4,16]{1,0:T(4,128)} %page_table.1) | copy-start | bytes 772
  0.7 1.6 %copy-start = (bf16[4,128,2048]{2,1,0:T(8,128)(2,1)S(1)}, bf16[4,128,2048]{2,1,0:T(8,128)(2,1)}, u32[]{:S(2)}) copy-start(bf16[4,128,2048]{2,1,0:T(8,128)(2,1)} %pool_in.1) | copy-start | bytes 6291460
  2.3 1.0 copy-start.1
  3.3 0.9 copy-start.3
  4.2 0.8 copy-start.4
  83.5 7.5 %copy-start.2 = (bf16[2,64,2048]{2,1,0:T(8,128)(2,1)S(1)}, bf16[2,64,2048]{2,1,0:T(8,128)(2,1)}, u32[]{:S(2)}) copy-start(bf16[2,64,2048]{2,1,0:T(8,128)(2,1)} %tokens.3) | copy-start | bytes 1572868
  83.5 7.5 %copy-start.5 = (f32[2048]{0:T(1024)S(1)}, f32[2048]{0:T(1024)}, u32[]{:S(2)}) copy-start(f32[2048]{0:T(1024)} %param.12) | copy-start | bytes 24580
  83.5 7.5 %copy-start.6 = (f32[2048]{0:T(1024)S(1)}, f32[2048]{0:T(1024)}, u32[]{:S(2)}) copy-start(f32[2048]{0:T(1024)} %param.13) | copy-start | bytes 24580

commit v5 on v1

v5 whole, which is shorter than its diff:
```python
import math

import jax
import jax.numpy as jnp
from jax import lax
from jax.experimental import pallas as pl
from jax.experimental.pallas import tpu as pltpu
from jax.sharding import PartitionSpec as P

HD = 128
NEG = -1e30
LN_EPS = 1e-06
LOG2E = 1.4426950408889634

NN = (((1,), (0,)), ((), ()))
NT = (((1,), (1,)), ((), ()))
TN = (((0,), (0,)), ((), ()))


def dot32(a, b, dims):
    return lax.dot_general(a, b, dims, preferred_element_type=jnp.float32)


def fold8(x, op):
    out = x[0:8]
    for i in range(1, x.shape[0] // 8):
        out = op(out, x[8 * i : 8 * i + 8])
    return out


MESH = pl.DeviceIdType.MESH


class Copies:
    def __init__(self):
        self.started = []

    def send(self, src, dst, send_sem, recv_sem, device_id):
        copy = pltpu.make_async_remote_copy(
            src_ref=src,
            dst_ref=dst,
            send_sem=send_sem,
            recv_sem=recv_sem,
            device_id=device_id,
            device_id_type=MESH,
        )
        copy.start()
        self.started.append(copy)

    def finish(self):
        for copy in self.started:
            copy.wait_send()


def await_copy(dst, recv_sem):
    pltpu.make_async_copy(dst, dst, recv_sem).wait()


def layer_kernel(
    page_table,
    prefix_len,
    group_of,
    tokens,
    w_ref,
    wo_ref,
    pool_in,
    gain,
    bias,
    hidden,
    cache,
    x_buf,
    wh,
    q2,
    kv,
    pool,
    wo,
    sc,
    scn,
    m_ref,
    l_ref,
    acc,
    o2,
    s2,
    o2_in,
    s2_in,
    at_out,
    at_in,
    mixed,
    tok,
    x_send,
    x_recv,
    w2_send,
    w2_recv,
    w3_send,
    w3_recv,
    p_send,
    p_recv,
    pz_send,
    pz_recv,
    c_send,
    c_recv,
    q_sem,
    local_sem,
    o1_send,
    o1_recv,
    o2_send,
    o2_recv,
    y_send,
    y_recv,
    a_send,
    a_recv,
):
    d = lax.axis_index("dp")
    f = lax.axis_index("fsdp")
    planes, owners = 8, 16
    heads = owners // 2
    y, h = f // heads, lax.rem(f, heads)
    x, core = h // 2, lax.rem(f, 2)
    z, z_pair = d // 2, lax.rem(d, 2)
    reqs, toks, width = tokens.shape
    rows = owners * toks
    slots, page, _ = pool_in.shape
    n_pages = page_table.shape[1]
    half_slots = heads * slots
    wq = w_ref.shape[0] // 4
    other_plane = 2 * z + 1 - z_pair
    up = lax.rem(d + 2, planes)
    down = lax.rem(d + planes - 2, planes)

    def at(yy, xx, cc):
        return (yy * 4 + lax.rem(xx, 4)) * 2 + cc

    def z_at(k):
        return lax.rem(z + k, 4)

    right, left = at(y, x + 1, core), at(y, x + 3, core)
    across, twin = at(1 - y, x, core), at(y, x, 1 - core)

    barrier = pltpu.get_barrier_semaphore()

    def greet(device_id):
        pl.semaphore_signal(barrier, inc=1, device_id=device_id, device_id_type=MESH)

    for k in range(1, owners):
        greet({"fsdp": lax.rem(f + k, owners)})
    for k in range(owners):
        greet({"dp": other_plane, "fsdp": lax.rem(f + k, owners)})
    greet({"dp": up})
    greet({"dp": down})
    for t in range(3):
        owner = (heads * t + h) // 3
        for r in range(heads):

            @pl.when((owner != d) | (h != r))
            def _():
                greet({"dp": owner, "fsdp": y * heads + r})

    holds_own = lax.rem(h + 3 * planes - 3 * d, heads) < 3
    own_x = pltpu.make_async_copy(tokens.at[y], x_buf.at[f], local_sem.at[1])
    own_x.start()
    own_tok = pltpu.make_async_copy(tokens, tok, local_sem.at[0])
    own_tok.start()
    pl.semaphore_wait(barrier, 2 * owners + 1 + 3 * planes - holds_own.astype(jnp.int32))

    out = Copies()
    w2_own = []
    for p in range(planes):
        plane = lax.rem(d + p, planes)
        zz = plane // 2
        for j in range(3):
            t, head = (3 * d + j) // heads, lax.rem(3 * d + j, heads)
            src = w_ref.at[pl.ds(pl.multiple_of(wq * zz, wq), wq), pl.ds(HD * j, HD)]
            dst = wh.at[f, zz, :, pl.ds(pl.multiple_of(HD * t, HD), HD)]
            if p:
                out.send(
                    src,
                    dst,
                    w2_send.at[p, j],
                    w2_recv.at[h, t],
                    {"dp": plane, "fsdp": y * heads + head},
                )
                continue

            @pl.when(head == h)
            def _():
                pltpu.make_async_copy(src, dst, w2_recv.at[h, t]).start()

            @pl.when(head != h)
            def _():
                pltpu.make_async_remote_copy(
                    src_ref=src,
                    dst_ref=dst,
                    send_sem=w2_send.at[0, j],
                    recv_sem=w2_recv.at[h, t],
                    device_id={"fsdp": y * heads + head},
                    device_id_type=MESH,
                ).start()

            w2_own.append((head, src, w2_send.at[0, j]))

    def send_x(n, src, who, dest):
        out.send(src, x_buf.at[who], x_send.at[n], x_recv.at[who], {"fsdp": dest})

    send_x(0, tokens.at[1 - y], f, across)
    send_x(1, tokens.at[y], f, right)
    send_x(2, tokens.at[y], f, left)
    send_x(3, tokens.at[y], f, twin)

    def pool_cols(t, head):
        return pl.ds(pl.multiple_of((t * heads + head) * HD, HD), HD)

    own_copies = []
    for t in range(2):
        cols = pl.ds(t * HD, HD)
        copy = pltpu.make_async_copy(
            pool_in.at[:, :, pool_cols(t, h)], pool.at[:, core, :, cols], local_sem.at[2 + t]
        )
        copy.start()
        own_copies.append(copy)
        out.send(
            pool_in.at[:, :, pool_cols(t, 2 * x + 1 - core)],
            pool.at[:, core, :, cols],
            p_send.at[0, t],
            p_recv.at[0, t],
            {"fsdp": twin},
        )
    for k in range(1, 4):
        for c in range(2):
            dest = at(y, x + k, c)
            place = 2 * (4 - k) + core
            for t in range(2):
                out.send(
                    pool_in.at[z, :, pool_cols(t, lax.rem(dest, heads))],
                    pool.at[z, place, :, pl.ds(t * HD, HD)],
                    p_send.at[2 * k + c, t],
                    p_recv.at[place, t],
                    {"fsdp": dest},
                )

    def wh_part(n, zz):
        row = y if n == 0 else 1 - y
        return wh.at[pl.ds(row * heads, heads), zz]

    def send_w(n, part, zz, dest):
        src = wh_part(part, zz)
        out.send(src, src, w3_send.at[n], w3_recv.at[zz, part], dest)

    for r in range(heads):
        for t in range(3):
            await_copy(wh.at[y * heads + r, z, :, pl.ds(HD * t, HD)], w2_recv.at[r, t])
    own_part = wh_part(0, z)
    out.send(own_part, own_part, w3_send.at[0], w3_recv.at[z, 1], {"fsdp": across})
    send_w(1, 0, z, {"dp": up})
    send_w(2, 0, z, {"dp": down})

    def pool_part(n, zz):
        return pool.at[zz, pl.ds(2 + 3 * n, 3)]

    def send_p(n, part, zz, dest):
        src = pool_part(part, zz)
        out.send(src, src, pz_send.at[n], pz_recv.at[zz, part], {"dp": dest})

    await_copy(x_buf.at[across], x_recv.at[across])
    send_x(4, x_buf.at[across], across, right)
    send_x(5, x_buf.at[across], across, left)
    send_x(6, x_buf.at[across], across, twin)
    a_left, b_left = at(y, x + 3, core), at(1 - y, x + 3, core)
    a_right, b_right = at(y, x + 1, core), at(1 - y, x + 1, core)
    a_far, b_far = at(y, x + 2, core), at(1 - y, x + 2, core)
    await_copy(x_buf.at[a_left], x_recv.at[a_left])
    send_x(7, x_buf.at[a_left], a_left, right)
    send_x(8, x_buf.at[a_left], a_left, twin)
    await_copy(x_buf.at[a_right], x_recv.at[a_right])
    send_x(9, x_buf.at[a_right], a_right, twin)
    await_copy(wh_part(1, z), w3_recv.at[z, 1])
    send_w(3, 1, z, {"dp": up})
    send_w(4, 1, z, {"dp": down})
    await_copy(wh_part(0, z_at(3)), w3_recv.at[z_at(3), 0])
    send_w(5, 0, z_at(3), {"dp": up})
    for place in range(2, 8):
        for t in range(2):
            await_copy(pool.at[z, place, :, pl.ds(t * HD, HD)], p_recv.at[place, t])
    for part in range(2):
        send_p(2 * part, part, z, up)
        send_p(2 * part + 1, part, z, down)
    await_copy(x_buf.at[b_right], x_recv.at[b_right])
    send_x(10, x_buf.at[b_right], b_right, left)
    send_x(11, x_buf.at[b_right], b_right, twin)
    await_copy(x_buf.at[b_left], x_recv.at[b_left])
    send_x(12, x_buf.at[b_left], b_left, twin)
    await_copy(wh_part(1, z_at(1)), w3_recv.at[z_at(1), 1])
    send_w(6, 1, z_at(1), {"dp": down})

    group = f // heads
    for p in range(2):
        for k in range(heads):
            dest = lax.rem(f // 2 + k, heads) * 2 + z_pair
            plane = d if p == 0 else other_plane
            sem = o1_send.at[p * heads + k]
            dst = wo.at[d, f]
            if p == 0 and k == 0:

                @pl.when(core == z_pair)
                def _():
                    pltpu.make_async_copy(wo_ref, dst, o1_recv.at[group]).start()

                @pl.when(core != z_pair)
                def _():
                    pltpu.make_async_remote_copy(
                        src_ref=wo_ref,
                        dst_ref=dst,
                        send_sem=sem,
                        recv_sem=o1_recv.at[group],
                        device_id={"fsdp": dest},
                        device_id_type=MESH,
                    ).start()

            else:
                out.send(wo_ref, dst, sem, o1_recv.at[group], {"dp": plane, "fsdp": dest})

    await_copy(pool_part(0, z_at(3)), pz_recv.at[z_at(3), 0])
    send_p(4, 0, z_at(3), up)
    await_copy(pool_part(1, z_at(1)), pz_recv.at[z_at(1), 1])
    send_p(5, 1, z_at(1), down)
    await_copy(x_buf.at[a_far], x_recv.at[a_far])
    send_x(13, x_buf.at[a_far], a_far, twin)
    await_copy(x_buf.at[b_far], x_recv.at[b_far])
    send_x(14, x_buf.at[b_far], b_far, twin)
    for yy in range(2):
        for xx in range(4):
            who = at(yy, xx, 1 - core)
            await_copy(x_buf.at[who], x_recv.at[who])
    own_x.wait()
    for k, part in ((1, 0), (3, 1), (2, 0), (2, 1)):
        await_copy(wh_part(part, z_at(k)), w3_recv.at[z_at(k), part])

    @pl.loop(0, owners // 4)
    def _(i):
        left_rows = x_buf[pl.ds(4 * i, 4)].reshape(4 * toks, width)
        got = dot32(left_rows, wh[...].reshape(width, 3 * HD), NN).astype(jnp.bfloat16)
        q2[0, pl.ds(pl.multiple_of(4 * i * toks, 4 * toks), 4 * toks), :] = got[:, :HD]
        kv[pl.ds(4 * i, 4)] = got[:, HD:].reshape(4, toks, 2 * HD)

    out.send(q2.at[0], q2.at[1], q_sem.at[0], q_sem.at[1], {"fsdp": across})

    def half(plane, n):
        return wo.at[plane, pl.ds(n * heads, heads)]

    def send_o(n, plane, part, dp, ff):
        src = half(plane, part)
        out.send(src, src, o2_send.at[n], o2_recv.at[plane, part], {"dp": dp, "fsdp": ff})

    def z_plane(k, c):
        return 2 * z_at(k) + c

    for part in range(2):
        plane = z_plane(0, core)
        await_copy(half(plane, part), o1_recv.at[part])
        send_o(3 * part, plane, part, up, f)
        send_o(3 * part + 1, plane, part, down, f)
        send_o(3 * part + 2, plane, part, d, twin)

    for k in range(owners):
        who = lax.rem(f + k, owners)
        for t in range(2):
            src = kv.at[who, :, pl.ds(t * HD, HD)]
            dst = cache.at[y, :, pool_cols(t, h)]
            if k == 0:
                copy = pltpu.make_async_copy(src, dst, local_sem.at[4 + t])
                copy.start()
                own_copies.append(copy)
            else:
                out.send(src, dst, c_send.at[k, t], c_recv.at[f, t], {"fsdp": who})

    for copy in own_copies[:2]:
        copy.wait()
    for t in range(2):
        await_copy(pool.at[:, 1 - core, :, pl.ds(t * HD, HD)], p_recv.at[0, t])
    for k, part in ((1, 0), (3, 1), (2, 0), (2, 1)):
        await_copy(pool_part(part, z_at(k)), pz_recv.at[z_at(k), part])

    inv_root = 1.0 / math.sqrt(HD)
    key_iota = lax.broadcasted_iota(jnp.int32, (page, rows), 0)

    def attend(j):
        req = y if j == 0 else 1 - y
        g = group_of[req]
        length = prefix_len[g]
        q = q2[j]

        def find(p):
            loc = page_table[g, p] - half_slots * y
            here = (loc >= 0) & (loc < half_slots)
            loc = jnp.clip(loc, 0, half_slots - 1)
            live = jnp.where(here, length - p * page, 0)
            return lax.rem(loc, slots), lax.rem(loc // slots + heads - 2 * x, heads), live

        m_ref[...] = jnp.full(m_ref.shape, NEG, jnp.float32)
        l_ref[...] = jnp.zeros(l_ref.shape, jnp.float32)
        acc[...] = jnp.zeros(acc.shape, jnp.float32)

        @pl.loop(0, n_pages)
        def _(p):
            a, b, live = find(p)
            s = dot32(pool[a, b, :, :HD], q, NT) * inv_root
            s = jnp.where(key_iota < live, s, NEG)
            sc[p] = s
            m_ref[...] = jnp.maximum(m_ref[...], fold8(s, jnp.maximum))

        if j == 0:
            for kb in range(rows // page):
                lo = kb * page
                keys = kv[2 * kb : 2 * kb + 2, :, :HD].reshape(page, HD)
                s = dot32(keys, q[lo:, :], NT) * inv_root
                ki = lax.broadcasted_iota(jnp.int32, s.shape, 0)
                qi = lax.broadcasted_iota(jnp.int32, s.shape, 1)
                s = jnp.where(ki <= qi, s, NEG)
                scn[kb, :, lo:] = s
                m_ref[:, lo:] = jnp.maximum(m_ref[:, lo:], fold8(s, jnp.maximum))
        top = jnp.maximum(jnp.max(m_ref[...], axis=0, keepdims=True), 0.5 * NEG)

        @pl.loop(0, n_pages // 2)
        def _(i):
            e = jnp.exp2((sc[pl.ds(2 * i, 2)].reshape(2 * page, rows) - top) * LOG2E)
            l_ref[...] += fold8(e, jnp.add)
            a, b, _ = find(2 * i)
            a1, b1, _ = find(2 * i + 1)
            values = jnp.concatenate([pool[a, b, :, HD:], pool[a1, b1, :, HD:]], 0)
            acc[...] += dot32(values, e.astype(jnp.bfloat16), TN)

        if j == 0:
            for kb in range(rows // page):
                lo = kb * page
                values = kv[2 * kb : 2 * kb + 2, :, HD:].reshape(page, HD)
                e = jnp.exp2((scn[kb, :, lo:] - top[:, lo:]) * LOG2E)
                l_ref[:, lo:] += fold8(e, jnp.add)
                acc[:, lo:] += dot32(values, e.astype(jnp.bfloat16), TN)
        return top, jnp.sum(l_ref[...], axis=0, keepdims=True)

    await_copy(q2.at[1], q_sem.at[1])
    top, total = attend(1)
    o2[...] = (acc[...] / jnp.maximum(total, 1.0)).astype(jnp.bfloat16)
    s2[0:1, :] = top
    s2[1:2, :] = total
    s2[2:8, :] = jnp.zeros((6, rows), jnp.float32)
    out.send(s2, s2_in, y_send.at[0], y_recv.at[0], {"fsdp": across})
    out.send(o2, o2_in, y_send.at[1], y_recv.at[1], {"fsdp": across})
    for n, (k, part) in enumerate(((3, 0), (1, 1), (1, 0), (3, 1))):
        plane = z_plane(k, core)
        await_copy(half(plane, part), o2_recv.at[plane, part])
        if n == 0:
            send_o(6, plane, part, up, f)
        if n == 1:
            send_o(7, plane, part, down, f)
        send_o(8 + n, plane, part, d, twin)

    top, total = attend(0)
    await_copy(s2_in, y_recv.at[0])
    await_copy(o2_in, y_recv.at[1])
    both = jnp.maximum(top, s2_in[0:1, :])
    f1 = jnp.exp(top - both)
    f2 = jnp.exp(s2_in[0:1, :] - both) * s2_in[1:2, :]
    attn = (acc[...] * f1 + o2_in[...].astype(jnp.float32) * f2) / (total * f1 + f2)
    at_out[...] = attn.T.astype(jnp.bfloat16).reshape(owners, toks, HD)
    at_in[y, :, pl.ds(pl.multiple_of(h * HD, HD), HD)] = at_out[f]
    for k in range(1, owners):
        who = lax.rem(f + k, owners)
        dst = at_in.at[y, :, pl.ds(pl.multiple_of(h * HD, HD), HD)]
        out.send(at_out.at[who], dst, a_send.at[k], a_recv.at[f], {"fsdp": who})
    for part in range(2):
        plane = z_plane(2, core)
        await_copy(half(plane, part), o2_recv.at[plane, part])
        send_o(12 + part, plane, part, d, twin)
    own_tok.wait()
    for k in range(1, owners):
        who = lax.rem(f + k, owners)
        col = pl.multiple_of(lax.rem(who, heads) * HD, HD)
        await_copy(at_in.at[who // heads, :, pl.ds(col, HD)], a_recv.at[who])
    for k in range(4):
        for part in range(2):
            plane = z_plane(k, 1 - core)
            await_copy(half(plane, part), o2_recv.at[plane, part])

    depth, cols = owners * wo.shape[2], wo.shape[3]
    left_rows = at_in[...].reshape(reqs * toks, depth)
    total = jnp.zeros((reqs * toks, 1), jnp.float32)
    for p in range(planes):
        part = dot32(left_rows, wo[p].reshape(depth, cols), NN)
        part = part + tok[:, :, p * cols : (p + 1) * cols].reshape(reqs * toks, cols).astype(
            jnp.float32
        )
        total = total + jnp.sum(part, axis=1, keepdims=True)
        mixed[:, p * cols : (p + 1) * cols] = part
    mean = total * (1.0 / width)
    square = jnp.zeros((reqs * toks, 1), jnp.float32)
    for p in range(planes):
        centred = mixed[:, p * cols : (p + 1) * cols] - mean
        square = square + jnp.sum(centred * centred, axis=1, keepdims=True)
    scale = lax.rsqrt(square * (1.0 / width) + LN_EPS)
    for p in range(planes):
        span = slice(p * cols, (p + 1) * cols)
        normed = (mixed[:, span] - mean) * scale * gain[0:1, span] + bias[0:1, span]
        hidden[:, :, span] = normed.astype(jnp.bfloat16).reshape(reqs, toks, cols)

    for copy in own_copies[2:]:
        copy.wait()
    for k in range(1, owners):
        who = lax.rem(f + k, owners)
        for t in range(2):
            await_copy(cache.at[who // heads, :, pool_cols(t, lax.rem(who, heads))], c_recv.at[who, t])

    @pl.when(core != z_pair)
    def _():
        await_copy(wo.at[d, f], o1_send.at[0])

    for head, src, sem in w2_own:

        @pl.when(head != h)
        def _():
            await_copy(src, sem)

    out.finish()


def body(tokens, w_qkv, w_out, ln_gain, ln_bias, kv_pool, page_table, prefix_len, group_of):
    reqs, toks, width = tokens.shape
    slots, page, _ = kv_pool.shape
    owners, planes, heads = 16, 8, 8
    rows = owners * toks
    dma = pltpu.SemaphoreType.DMA
    hbm = pl.BlockSpec(memory_space=pltpu.HBM)
    vmem = pl.BlockSpec(memory_space=pltpu.VMEM)
    smem = pl.BlockSpec(memory_space=pltpu.SMEM)
    bf16, f32 = jnp.bfloat16, jnp.float32
    return pl.pallas_call(
        layer_kernel,
        out_shape=(
            jax.ShapeDtypeStruct(tokens.shape, bf16),
            jax.ShapeDtypeStruct((reqs, toks, 2 * heads * HD), bf16),
        ),
        in_specs=[smem, smem, smem, hbm, hbm, hbm, hbm, vmem, vmem],
        out_specs=(vmem, hbm),
        scratch_shapes=[
            pltpu.VMEM((owners, toks, width), bf16),
            pltpu.VMEM((owners, 4, w_qkv.shape[0] // 4, 3 * HD), bf16),
            pltpu.VMEM((2, rows, HD), bf16),
            pltpu.VMEM((owners, toks, 2 * HD), bf16),
            pltpu.VMEM((slots, heads, page, 2 * HD), bf16),
            pltpu.VMEM((planes, owners) + w_out.shape, bf16),
            pltpu.VMEM((page_table.shape[1], page, rows), f32),
            pltpu.VMEM((rows // page, page, rows), f32),
            pltpu.VMEM((8, rows), f32),
            pltpu.VMEM((8, rows), f32),
            pltpu.VMEM((HD, rows), f32),
            pltpu.VMEM((HD, rows), bf16),
            pltpu.VMEM((8, rows), f32),
            pltpu.VMEM((HD, rows), bf16),
            pltpu.VMEM((8, rows), f32),
            pltpu.VMEM((owners, toks, HD), bf16),
            pltpu.VMEM((reqs, toks, heads * HD), bf16),
            pltpu.VMEM((reqs * toks, width), f32),
            pltpu.VMEM(tokens.shape, bf16),
            dma((15,)),
            dma((owners,)),
            dma((planes, 3)),
            dma((heads, 3)),
            dma((7,)),
            dma((4, 2)),
            dma((heads, 2)),
            dma((heads, 2)),
            dma((6,)),
            dma((4, 2)),
            dma((owners, 2)),
            dma((owners, 2)),
            dma((2,)),
            dma((6,)),
            dma((owners,)),
            dma((2,)),
            dma((15,)),
            dma((planes, 2)),
            dma((2,)),
            dma((2,)),
            dma((owners,)),
            dma((owners,)),
        ],
        compiler_params=pltpu.CompilerParams(
            collective_id=0, has_side_effects=True, vmem_limit_bytes=67043328
        ),
        name="layer",
    )(
        page_table,
        prefix_len,
        group_of,
        tokens,
        w_qkv,
        w_out,
        kv_pool,
        ln_gain.reshape(1, width),
        ln_bias.reshape(1, width),
    )


def solution(mesh):
    in_specs = (
        P("dp", "fsdp", None),
        P("fsdp", "dp"),
        P("fsdp", "dp"),
        P(),
        P(),
        P("fsdp", None, None),
        P(),
        P(),
        P("dp"),
    )
    out_specs = (P("dp", "fsdp", None), P("dp", "fsdp", None))
    return jax.shard_map(body, mesh=mesh, in_specs=in_specs, out_specs=out_specs, check_vma=False)
```

time: 266 us -> 88.1 us (0.33)
  waiting for transfers between devices: 96.8 us -> 0 us
  Pallas kernels: 6.24 us -> 83.5 us
  blocking collectives: 74.9 us -> 0 us
  starting transfers between devices: 45.9 us -> 0 us
  between operations: 14.3 us -> 0.64 us
  local copies, waits for them, and re-layouts: 15.4 us -> 3.76 us
  matrix products: 8 us -> 0 us
    all_to_all x5 -> x0, waiting for transfers between devices: 89.7 us -> none  [the longest x1 63.8 us: body(): mine = lax.all_to_all(sent, 'fsdp', 0, 0, tiled=True).reshape(rows, width)]
    pallas_call x1, Pallas kernels: 6.24 us -> 83.5 us  [body(): pl.pallas_call(layer_kernel, out_shape=(jax.ShapeDtypeStruct(tokens.shape...]
    all_gather x2 -> x0, blocking collectives: 74.9 us -> none  [the longest x1 41.2 us: body(): lax.all_gather(w_out, 'dp', axis=1, tiled=True)]
    all_to_all x5 -> x0, starting transfers between devices: 42.3 us -> none  [the longest x1 16.8 us: body(): mine = lax.all_to_all(sent, 'fsdp', 0, 0, tiled=True).reshape(rows, width)]
    dot_general x2 -> x0, matrix products: 8 us -> none  [the longest x1 4.99 us: body(): jnp.dot(mine, wh, preferred_element_type=jnp.float32).astype(jnp.bfloat16)]
    ppermute x3 -> x0, waiting for transfers between devices: 7.07 us -> none  [the longest x1 6.68 us: body(): q_par = lax.ppermute(q, 'fsdp', flip)]
    reshape x6 -> x0, local copies, waits for them, and re-layouts: 6.25 us -> none  [the longest x1 2.69 us: body(): ps.reshape(heads, slots, page, 2 * HD)]
    ppermute x3 -> x0, starting transfers between devices: 3.54 us -> none  [the longest x1 2.07 us: body(): q_par = lax.ppermute(q, 'fsdp', flip)]
  transfers between devices with their start and end apart: 9 -> 0, of which waited for: 6 -> 0; matrix products, arithmetic and copies ran while one was open for 6% -> 0% of each run, Pallas kernels for 2% -> 0%
where the time goes in v5:
time: 88.1 us; the launch traced here: 87.9 us
  Pallas kernels  83.5 us (95%)
  local copies, waits for them, and re-layouts  3.76 us (4%)
    pallas_call x1, Pallas kernels, body(): pl.pallas_call(layer_kernel, out_shape=(jax.ShapeDtypeStruct(tokens.shape...  83.5 us
    unnamed x2, local copies, waits for them, and re-layouts  3.76 us

profile of v5, /device:TPU:1, one launch (start us, length us, event | category | flops | bytes accessed | tf_op | source)
XLA Modules:
  0.0 87.9 jit_solution(322232985176743703)
XLA Ops:
  0.6 83.5 %layer.1 = (bf16[2,64,2048]{2,1,0:T(8,128)(2,1)}, bf16[2,64,2048]{2,1,0:T(8,128)(2,1)}) custom-call(s32[4,16]{1,0:T(4,128)} %page_table.1, s32[4]{0:T(128)} %prefix_len.1, s32[2]{0:T(128)} %group_of.1, bf16[2,64,2048]{2,1,0:T(8,128)(2,1)} %tokens.1, bf16[128,384]{1,0:T(8,128)(2,1)} %w_ref.1, bf16[64,256]{1,0:T(8,128)(2,1)} %wo_ref.1, ...), custom_call_target="tpu_custom_call" | custom-call | tf_op jit(solution)/shard_map/layer/pallas_call | solution.py:535
  84.1 1.9 %copy.13 = bf16[2,64,2048]{2,1,0:T(8,128)(2,1)} copy(bf16[2,64,2048]{2,1,0:T(8,128)(2,1)} %get-tuple-element.4) | data formatting | bytes 1048576
  86.0 1.9 %copy.14 = bf16[2,64,2048]{2,1,0:T(8,128)(2,1)} copy(bf16[2,64,2048]{2,1,0:T(8,128)(2,1)} %get-tuple-element.5) | data formatting | bytes 1048576

commit v6 on v5

--- a/solution.py
+++ b/solution.py
@@ -74,11 +74,15 @@
     kv,
     pool,
     wo,
+    wo_both,
     sc,
     scn,
     m_ref,
     l_ref,
     acc,
+    m_other,
+    l_other,
+    acc_other,
     o2,
     s2,
     o2_in,
@@ -99,8 +103,11 @@
     pz_recv,
     c_send,
     c_recv,
-    q_sem,
+    q_send,
+    q_recv,
     local_sem,
+    o0_send,
+    o0_recv,
     o1_send,
     o1_recv,
     o2_send,
@@ -143,8 +150,7 @@
 
     for k in range(1, owners):
         greet({"fsdp": lax.rem(f + k, owners)})
-    for k in range(owners):
-        greet({"dp": other_plane, "fsdp": lax.rem(f + k, owners)})
+    greet({"dp": other_plane})
     greet({"dp": up})
     greet({"dp": down})
     for t in range(3):
@@ -160,7 +166,9 @@
     own_x.start()
     own_tok = pltpu.make_async_copy(tokens, tok, local_sem.at[0])
     own_tok.start()
-    pl.semaphore_wait(barrier, 2 * owners + 1 + 3 * planes - holds_own.astype(jnp.int32))
+    own_wo = pltpu.make_async_copy(wo_ref, wo_both.at[z_pair], local_sem.at[6])
+    own_wo.start()
+    pl.semaphore_wait(barrier, owners + 2 + 3 * planes - holds_own.astype(jnp.int32))
 
     out = Copies()
     w2_own = []
@@ -198,13 +206,26 @@
 
             w2_own.append((head, src, w2_send.at[0, j]))
 
-    def send_x(n, src, who, dest):
-        out.send(src, x_buf.at[who], x_send.at[n], x_recv.at[who], {"fsdp": dest})
-
-    send_x(0, tokens.at[1 - y], f, across)
-    send_x(1, tokens.at[y], f, right)
-    send_x(2, tokens.at[y], f, left)
-    send_x(3, tokens.at[y], f, twin)
+    half_toks = toks // 2
+
+    def send_x(n, src, who, part, dest):
+        dst = x_buf.at[who, pl.ds(part * half_toks, half_toks)]
+        out.send(
+            dst if src is None else src.at[pl.ds(part * half_toks, half_toks)],
+            dst,
+            x_send.at[n, part],
+            x_recv.at[who, part],
+            {"fsdp": dest},
+        )
+
+    def await_x(who, part):
+        await_copy(x_buf.at[who, pl.ds(part * half_toks, half_toks)], x_recv.at[who, part])
+
+    for part in range(2):
+        send_x(0, tokens.at[1 - y], f, part, across)
+        send_x(1, tokens.at[y], f, part, right)
+        send_x(2, tokens.at[y], f, part, left)
+        send_x(3, tokens.at[y], f, part, twin)
 
     def pool_cols(t, head):
         return pl.ds(pl.multiple_of((t * heads + head) * HD, HD), HD)
@@ -260,88 +281,86 @@
         src = pool_part(part, zz)
         out.send(src, src, pz_send.at[n], pz_recv.at[zz, part], {"dp": dest})
 
-    await_copy(x_buf.at[across], x_recv.at[across])
-    send_x(4, x_buf.at[across], across, right)
-    send_x(5, x_buf.at[across], across, left)
-    send_x(6, x_buf.at[across], across, twin)
     a_left, b_left = at(y, x + 3, core), at(1 - y, x + 3, core)
     a_right, b_right = at(y, x + 1, core), at(1 - y, x + 1, core)
     a_far, b_far = at(y, x + 2, core), at(1 - y, x + 2, core)
-    await_copy(x_buf.at[a_left], x_recv.at[a_left])
-    send_x(7, x_buf.at[a_left], a_left, right)
-    send_x(8, x_buf.at[a_left], a_left, twin)
-    await_copy(x_buf.at[a_right], x_recv.at[a_right])
-    send_x(9, x_buf.at[a_right], a_right, twin)
+    for part in range(2):
+        await_x(across, part)
+        send_x(4, None, across, part, right)
+        send_x(5, None, across, part, left)
+        send_x(6, None, across, part, twin)
+    for part in range(2):
+        await_x(a_left, part)
+        send_x(7, None, a_left, part, right)
+        send_x(8, None, a_left, part, twin)
+        await_x(a_right, part)
+        send_x(9, None, a_right, part, twin)
+    await_copy(wh_part(0, z_at(3)), w3_recv.at[z_at(3), 0])
+    send_w(5, 0, z_at(3), {"dp": up})
     await_copy(wh_part(1, z), w3_recv.at[z, 1])
     send_w(3, 1, z, {"dp": up})
     send_w(4, 1, z, {"dp": down})
-    await_copy(wh_part(0, z_at(3)), w3_recv.at[z_at(3), 0])
-    send_w(5, 0, z_at(3), {"dp": up})
+    out.send(wo_ref, wo_both.at[z_pair], o0_send, o0_recv, {"dp": other_plane})
     for place in range(2, 8):
         for t in range(2):
             await_copy(pool.at[z, place, :, pl.ds(t * HD, HD)], p_recv.at[place, t])
-    for part in range(2):
-        send_p(2 * part, part, z, up)
-        send_p(2 * part + 1, part, z, down)
-    await_copy(x_buf.at[b_right], x_recv.at[b_right])
-    send_x(10, x_buf.at[b_right], b_right, left)
-    send_x(11, x_buf.at[b_right], b_right, twin)
-    await_copy(x_buf.at[b_left], x_recv.at[b_left])
-    send_x(12, x_buf.at[b_left], b_left, twin)
+    send_p(0, 0, z, up)
+    send_p(1, 1, z, up)
+    for part in range(2):
+        await_x(b_right, part)
+        send_x(10, None, b_right, part, left)
+        send_x(11, None, b_right, part, twin)
+        await_x(b_left, part)
+        send_x(12, None, b_left, part, twin)
     await_copy(wh_part(1, z_at(1)), w3_recv.at[z_at(1), 1])
     send_w(6, 1, z_at(1), {"dp": down})
+    send_p(2, 1, z, down)
+    send_p(3, 0, z, down)
 
     group = f // heads
-    for p in range(2):
-        for k in range(heads):
-            dest = lax.rem(f // 2 + k, heads) * 2 + z_pair
-            plane = d if p == 0 else other_plane
-            sem = o1_send.at[p * heads + k]
-            dst = wo.at[d, f]
-            if p == 0 and k == 0:
-
-                @pl.when(core == z_pair)
-                def _():
-                    pltpu.make_async_copy(wo_ref, dst, o1_recv.at[group]).start()
-
-                @pl.when(core != z_pair)
-                def _():
-                    pltpu.make_async_remote_copy(
-                        src_ref=wo_ref,
-                        dst_ref=dst,
-                        send_sem=sem,
-                        recv_sem=o1_recv.at[group],
-                        device_id={"fsdp": dest},
-                        device_id_type=MESH,
-                    ).start()
-
-            else:
-                out.send(wo_ref, dst, sem, o1_recv.at[group], {"dp": plane, "fsdp": dest})
+    own_wo.wait()
+    await_copy(wo_both.at[1 - z_pair], o0_recv)
+    pltpu.make_async_copy(wo_both.at[core], wo.at[2 * z + core, f], o1_recv.at[group]).start()
+    for k in range(1, owners):
+        dest = lax.rem(f + k, owners)
+        c = lax.rem(dest, 2)
+        out.send(
+            wo_both.at[c], wo.at[2 * z + c, f], o1_send.at[k], o1_recv.at[group], {"fsdp": dest}
+        )
 
     await_copy(pool_part(0, z_at(3)), pz_recv.at[z_at(3), 0])
     send_p(4, 0, z_at(3), up)
     await_copy(pool_part(1, z_at(1)), pz_recv.at[z_at(1), 1])
     send_p(5, 1, z_at(1), down)
-    await_copy(x_buf.at[a_far], x_recv.at[a_far])
-    send_x(13, x_buf.at[a_far], a_far, twin)
-    await_copy(x_buf.at[b_far], x_recv.at[b_far])
-    send_x(14, x_buf.at[b_far], b_far, twin)
-    for yy in range(2):
-        for xx in range(4):
-            who = at(yy, xx, 1 - core)
-            await_copy(x_buf.at[who], x_recv.at[who])
-    own_x.wait()
+    for part in range(2):
+        await_x(a_far, part)
+        send_x(13, None, a_far, part, twin)
     for k, part in ((1, 0), (3, 1), (2, 0), (2, 1)):
         await_copy(wh_part(part, z_at(k)), w3_recv.at[z_at(k), part])
-
-    @pl.loop(0, owners // 4)
-    def _(i):
-        left_rows = x_buf[pl.ds(4 * i, 4)].reshape(4 * toks, width)
-        got = dot32(left_rows, wh[...].reshape(width, 3 * HD), NN).astype(jnp.bfloat16)
-        q2[0, pl.ds(pl.multiple_of(4 * i * toks, 4 * toks), 4 * toks), :] = got[:, :HD]
-        kv[pl.ds(4 * i, 4)] = got[:, HD:].reshape(4, toks, 2 * HD)
-
-    out.send(q2.at[0], q2.at[1], q_sem.at[0], q_sem.at[1], {"fsdp": across})
+    for part in range(2):
+        await_x(b_far, part)
+        send_x(14, None, b_far, part, twin)
+    own_x.wait()
+
+    span = rows // 2
+    for k in range(2):
+        row = y if k == 0 else 1 - y
+        for xx in range(4):
+            for part in range(2):
+                await_x(at(row, xx, 1 - core), part)
+
+        @pl.loop(0, 2)
+        def _(i):
+            first = row * heads + 4 * i
+            left_rows = x_buf[pl.ds(first, 4)].reshape(4 * toks, width)
+            got = dot32(left_rows, wh[...].reshape(width, 3 * HD), NN).astype(jnp.bfloat16)
+            q2[0, pl.ds(pl.multiple_of(first * toks, 4 * toks), 4 * toks), :] = got[:, :HD]
+            kv[pl.ds(first, 4)] = got[:, HD:].reshape(4, toks, 2 * HD)
+
+        at_rows = pl.ds(pl.multiple_of(row * span, span), span)
+        out.send(
+            q2.at[0, at_rows], q2.at[1, at_rows], q_send.at[k], q_recv.at[k], {"fsdp": across}
+        )
 
     def half(plane, n):
         return wo.at[plane, pl.ds(n * heads, heads)]
@@ -353,13 +372,116 @@
     def z_plane(k, c):
         return 2 * z_at(k) + c
 
-    for part in range(2):
-        plane = z_plane(0, core)
+    plane = z_plane(0, core)
+    for part in range(2):
         await_copy(half(plane, part), o1_recv.at[part])
-        send_o(3 * part, plane, part, up, f)
-        send_o(3 * part + 1, plane, part, down, f)
-        send_o(3 * part + 2, plane, part, d, twin)
-
+    send_o(0, plane, 0, up, f)
+    send_o(1, plane, 1, down, f)
+    send_o(2, plane, 1, up, f)
+    send_o(3, plane, 0, down, f)
+    for part in range(2):
+        send_o(4 + part, plane, part, d, twin)
+
+    inv_root = 1.0 / math.sqrt(HD)
+    key_iota = lax.broadcasted_iota(jnp.int32, (page, span), 0)
+    query_iota = lax.broadcasted_iota(jnp.int32, (page, span), 1)
+
+    def put(index, scores, live, m_at):
+        for n in range(2):
+            part = jnp.where(live[n], scores[n * page : (n + 1) * page], NEG)
+            m_at[...] = jnp.maximum(m_at[...], fold8(part, jnp.maximum))
+            index(n)[...] = part
+
+    def add(scores, values, top, l_at, acc_at):
+        e = jnp.exp2((scores.reshape(2 * page, span) - top) * LOG2E)
+        l_at[...] += fold8(e, jnp.add)
+        acc_at[...] += dot32(values, e.astype(jnp.bfloat16), TN)
+
+    def highest(m_at):
+        return jnp.maximum(jnp.max(m_at[...], axis=0, keepdims=True), 0.5 * NEG)
+
+    def pages(j, hh):
+        g = group_of[y if j == 0 else 1 - y]
+        length = prefix_len[g]
+
+        def find(p):
+            loc = page_table[g, p] - half_slots * y
+            here = (loc >= 0) & (loc < half_slots)
+            loc = jnp.clip(loc, 0, half_slots - 1)
+            live = jnp.where(here, length - p * page, 0)
+            return lax.rem(loc, slots), lax.rem(loc // slots + heads - 2 * x, heads), live
+
+        def both(i, cols):
+            a, b, live_a = find(2 * i)
+            c, e, live_b = find(2 * i + 1)
+            return jnp.concatenate([pool[a, b, :, cols], pool[c, e, :, cols]], 0), (live_a, live_b)
+
+        def scores(q, m_at):
+            @pl.loop(0, n_pages // 2)
+            def _(i):
+                keys, live = both(i, slice(0, HD))
+                put(
+                    lambda n: sc.at[2 * i + n],
+                    dot32(keys, q, NT) * inv_root,
+                    [key_iota < live[0], key_iota < live[1]],
+                    m_at,
+                )
+
+        def sums(top, l_at, acc_at):
+            @pl.loop(0, n_pages // 2)
+            def _(i):
+                values, _ = both(i, slice(HD, 2 * HD))
+                add(sc[pl.ds(2 * i, 2)], values, top, l_at, acc_at)
+
+        return scores, sums
+
+    def queries(j, hh):
+        return q2[j, pl.ds(pl.multiple_of(hh * span, span), span), :]
+
+    m_ref[...] = jnp.full(m_ref.shape, NEG, jnp.float32)
+    l_ref[...] = jnp.zeros(l_ref.shape, jnp.float32)
+    acc[...] = jnp.zeros(acc.shape, jnp.float32)
+    pairs = span // (2 * page)
+    for hh in range(2):
+        q = queries(0, hh)
+
+        @pl.loop(0, pairs * (hh + 1))
+        def _(i):
+            keys = kv[pl.ds(4 * i, 4), :, :HD].reshape(2 * page, HD)
+            ahead = [
+                key_iota + (2 * i + n) * page <= query_iota + hh * span for n in range(2)
+            ]
+            put(
+                lambda n: scn.at[hh, 2 * i + n], dot32(keys, q, NT) * inv_root, ahead, m_ref.at[hh]
+            )
+
+    for copy in own_copies:
+        copy.wait()
+    for t in range(2):
+        await_copy(pool.at[:, 1 - core, :, pl.ds(t * HD, HD)], p_recv.at[0, t])
+    for k, part in ((1, 0), (3, 1), (2, 0), (2, 1)):
+        await_copy(pool_part(part, z_at(k)), pz_recv.at[z_at(k), part])
+
+    for k in range(2):
+        hh = 1 - y if k == 0 else y
+        await_copy(q2.at[1, pl.ds(pl.multiple_of(hh * span, span), span)], q_recv.at[k])
+        q = queries(1, hh)
+        scores, sums = pages(1, hh)
+        m_other[...] = jnp.full(m_other.shape, NEG, jnp.float32)
+        l_other[...] = jnp.zeros(l_other.shape, jnp.float32)
+        acc_other[...] = jnp.zeros(acc_other.shape, jnp.float32)
+        scores(q, m_other)
+        top = highest(m_other)
+        sums(top, l_other, acc_other)
+        total = jnp.sum(l_other[...], axis=0, keepdims=True)
+        o2[k] = (acc_other[...] / jnp.maximum(total, 1.0)).astype(jnp.bfloat16)
+        s2[k, 0:1, :] = top
+        s2[k, 1:2, :] = total
+        s2[k, 2:8, :] = jnp.zeros((6, span), jnp.float32)
+        out.send(s2.at[k], s2_in.at[k], y_send.at[0, k], y_recv.at[0, k], {"fsdp": across})
+        out.send(o2.at[k], o2_in.at[k], y_send.at[1, k], y_recv.at[1, k], {"fsdp": across})
+
+    own_cache = []
     for k in range(owners):
         who = lax.rem(f + k, owners)
         for t in range(2):
@@ -368,105 +490,49 @@
             if k == 0:
                 copy = pltpu.make_async_copy(src, dst, local_sem.at[4 + t])
                 copy.start()
-                own_copies.append(copy)
+                own_cache.append(copy)
             else:
                 out.send(src, dst, c_send.at[k, t], c_recv.at[f, t], {"fsdp": who})
 
-    for copy in own_copies[:2]:
-        copy.wait()
-    for t in range(2):
-        await_copy(pool.at[:, 1 - core, :, pl.ds(t * HD, HD)], p_recv.at[0, t])
-    for k, part in ((1, 0), (3, 1), (2, 0), (2, 1)):
-        await_copy(pool_part(part, z_at(k)), pz_recv.at[z_at(k), part])
-
-    inv_root = 1.0 / math.sqrt(HD)
-    key_iota = lax.broadcasted_iota(jnp.int32, (page, rows), 0)
-
-    def attend(j):
-        req = y if j == 0 else 1 - y
-        g = group_of[req]
-        length = prefix_len[g]
-        q = q2[j]
-
-        def find(p):
-            loc = page_table[g, p] - half_slots * y
-            here = (loc >= 0) & (loc < half_slots)
-            loc = jnp.clip(loc, 0, half_slots - 1)
-            live = jnp.where(here, length - p * page, 0)
-            return lax.rem(loc, slots), lax.rem(loc // slots + heads - 2 * x, heads), live
-
-        m_ref[...] = jnp.full(m_ref.shape, NEG, jnp.float32)
-        l_ref[...] = jnp.zeros(l_ref.shape, jnp.float32)
-        acc[...] = jnp.zeros(acc.shape, jnp.float32)
-
-        @pl.loop(0, n_pages)
-        def _(p):
-            a, b, live = find(p)
-            s = dot32(pool[a, b, :, :HD], q, NT) * inv_root
-            s = jnp.where(key_iota < live, s, NEG)
-            sc[p] = s
-            m_ref[...] = jnp.maximum(m_ref[...], fold8(s, jnp.maximum))
-
-        if j == 0:
-            for kb in range(rows // page):
-                lo = kb * page
-                keys = kv[2 * kb : 2 * kb + 2, :, :HD].reshape(page, HD)
-                s = dot32(keys, q[lo:, :], NT) * inv_root
-                ki = lax.broadcasted_iota(jnp.int32, s.shape, 0)
-                qi = lax.broadcasted_iota(jnp.int32, s.shape, 1)
-                s = jnp.where(ki <= qi, s, NEG)
-                scn[kb, :, lo:] = s
-                m_ref[:, lo:] = jnp.maximum(m_ref[:, lo:], fold8(s, jnp.maximum))
-        top = jnp.maximum(jnp.max(m_ref[...], axis=0, keepdims=True), 0.5 * NEG)
-
-        @pl.loop(0, n_pages // 2)
-        def _(i):
-            e = jnp.exp2((sc[pl.ds(2 * i, 2)].reshape(2 * page, rows) - top) * LOG2E)
-            l_ref[...] += fold8(e, jnp.add)
-            a, b, _ = find(2 * i)
-            a1, b1, _ = find(2 * i + 1)
-            values = jnp.concatenate([pool[a, b, :, HD:], pool[a1, b1, :, HD:]], 0)
-            acc[...] += dot32(values, e.astype(jnp.bfloat16), TN)
-
-        if j == 0:
-            for kb in range(rows // page):
-                lo = kb * page
-                values = kv[2 * kb : 2 * kb + 2, :, HD:].reshape(page, HD)
-                e = jnp.exp2((scn[kb, :, lo:] - top[:, lo:]) * LOG2E)
-                l_ref[:, lo:] += fold8(e, jnp.add)
-                acc[:, lo:] += dot32(values, e.astype(jnp.bfloat16), TN)
-        return top, jnp.sum(l_ref[...], axis=0, keepdims=True)
-
-    await_copy(q2.at[1], q_sem.at[1])
-    top, total = attend(1)
-    o2[...] = (acc[...] / jnp.maximum(total, 1.0)).astype(jnp.bfloat16)
-    s2[0:1, :] = top
-    s2[1:2, :] = total
-    s2[2:8, :] = jnp.zeros((6, rows), jnp.float32)
-    out.send(s2, s2_in, y_send.at[0], y_recv.at[0], {"fsdp": across})
-    out.send(o2, o2_in, y_send.at[1], y_recv.at[1], {"fsdp": across})
-    for n, (k, part) in enumerate(((3, 0), (1, 1), (1, 0), (3, 1))):
+    for n, (k, part) in enumerate(((3, 0), (1, 1))):
         plane = z_plane(k, core)
         await_copy(half(plane, part), o2_recv.at[plane, part])
-        if n == 0:
-            send_o(6, plane, part, up, f)
-        if n == 1:
-            send_o(7, plane, part, down, f)
+        send_o(6 + n, plane, part, down if n else up, f)
         send_o(8 + n, plane, part, d, twin)
 
-    top, total = attend(0)
-    await_copy(s2_in, y_recv.at[0])
-    await_copy(o2_in, y_recv.at[1])
-    both = jnp.maximum(top, s2_in[0:1, :])
-    f1 = jnp.exp(top - both)
-    f2 = jnp.exp(s2_in[0:1, :] - both) * s2_in[1:2, :]
-    attn = (acc[...] * f1 + o2_in[...].astype(jnp.float32) * f2) / (total * f1 + f2)
-    at_out[...] = attn.T.astype(jnp.bfloat16).reshape(owners, toks, HD)
-    at_in[y, :, pl.ds(pl.multiple_of(h * HD, HD), HD)] = at_out[f]
-    for k in range(1, owners):
-        who = lax.rem(f + k, owners)
-        dst = at_in.at[y, :, pl.ds(pl.multiple_of(h * HD, HD), HD)]
-        out.send(at_out.at[who], dst, a_send.at[k], a_recv.at[f], {"fsdp": who})
+    for k in range(2):
+        hh = y if k == 0 else 1 - y
+        q = queries(0, hh)
+        scores, sums = pages(0, hh)
+        scores(q, m_ref.at[hh])
+        top = highest(m_ref.at[hh])
+        sums(top, l_ref.at[hh], acc.at[hh])
+
+        @pl.loop(0, pairs * (hh + 1))
+        def _(i):
+            values = kv[pl.ds(4 * i, 4), :, HD:].reshape(2 * page, HD)
+            add(scn[hh, pl.ds(2 * i, 2)], values, top, l_ref.at[hh], acc.at[hh])
+
+        total = jnp.sum(l_ref[hh], axis=0, keepdims=True)
+        await_copy(s2_in.at[k], y_recv.at[0, k])
+        await_copy(o2_in.at[k], y_recv.at[1, k])
+        both_top = jnp.maximum(top, s2_in[k, 0:1, :])
+        f1 = jnp.exp(top - both_top)
+        f2 = jnp.exp(s2_in[k, 0:1, :] - both_top) * s2_in[k, 1:2, :]
+        attn = (acc[hh] * f1 + o2_in[k].astype(jnp.float32) * f2) / (total * f1 + f2)
+        at_out[pl.ds(hh * heads, heads)] = attn.T.astype(jnp.bfloat16).reshape(heads, toks, HD)
+        col = pl.ds(pl.multiple_of(h * HD, HD), HD)
+        if k == 0:
+            at_in[y, :, col] = at_out[f]
+        for i in range(1 - k, heads):
+            who = hh * heads + lax.rem(h + i, heads)
+            n = k * heads + i
+            out.send(at_out.at[who], at_in.at[y, :, col], a_send.at[n], a_recv.at[f], {"fsdp": who})
+        if k == 0:
+            for n, (kk, part) in enumerate(((1, 0), (3, 1))):
+                plane = z_plane(kk, core)
+                await_copy(half(plane, part), o2_recv.at[plane, part])
+                send_o(10 + n, plane, part, d, twin)
     for part in range(2):
         plane = z_plane(2, core)
         await_copy(half(plane, part), o2_recv.at[plane, part])
@@ -502,16 +568,12 @@
         normed = (mixed[:, span] - mean) * scale * gain[0:1, span] + bias[0:1, span]
         hidden[:, :, span] = normed.astype(jnp.bfloat16).reshape(reqs, toks, cols)
 
-    for copy in own_copies[2:]:
+    for copy in own_cache:
         copy.wait()
     for k in range(1, owners):
         who = lax.rem(f + k, owners)
         for t in range(2):
             await_copy(cache.at[who // heads, :, pool_cols(t, lax.rem(who, heads))], c_recv.at[who, t])
-
-    @pl.when(core != z_pair)
-    def _():
-        await_copy(wo.at[d, f], o1_send.at[0])
 
     for head, src, sem in w2_own:
 
@@ -547,21 +609,25 @@
             pltpu.VMEM((owners, toks, 2 * HD), bf16),
             pltpu.VMEM((slots, heads, page, 2 * HD), bf16),
             pltpu.VMEM((planes, owners) + w_out.shape, bf16),
-            pltpu.VMEM((page_table.shape[1], page, rows), f32),
-            pltpu.VMEM((rows // page, page, rows), f32),
-            pltpu.VMEM((8, rows), f32),
-            pltpu.VMEM((8, rows), f32),
-            pltpu.VMEM((HD, rows), f32),
-            pltpu.VMEM((HD, rows), bf16),
-            pltpu.VMEM((8, rows), f32),
-            pltpu.VMEM((HD, rows), bf16),
-            pltpu.VMEM((8, rows), f32),
+            pltpu.VMEM((2,) + w_out.shape, bf16),
+            pltpu.VMEM((page_table.shape[1], page, rows // 2), f32),
+            pltpu.VMEM((2, rows // page, page, rows // 2), f32),
+            pltpu.VMEM((2, 8, rows // 2), f32),
+            pltpu.VMEM((2, 8, rows // 2), f32),
+            pltpu.VMEM((2, HD, rows // 2), f32),
+            pltpu.VMEM((8, rows // 2), f32),
+            pltpu.VMEM((8, rows // 2), f32),
+            pltpu.VMEM((HD, rows // 2), f32),
+            pltpu.VMEM((2, HD, rows // 2), bf16),
+            pltpu.VMEM((2, 8, rows // 2), f32),
+            pltpu.VMEM((2, HD, rows // 2), bf16),
+            pltpu.VMEM((2, 8, rows // 2), f32),
             pltpu.VMEM((owners, toks, HD), bf16),
             pltpu.VMEM((reqs, toks, heads * HD), bf16),
             pltpu.VMEM((reqs * toks, width), f32),
             pltpu.VMEM(tokens.shape, bf16),
-            dma((15,)),
-            dma((owners,)),
+            dma((15, 2)),
+            dma((owners, 2)),
             dma((planes, 3)),
             dma((heads, 3)),
             dma((7,)),
@@ -573,13 +639,16 @@
             dma((owners, 2)),
             dma((owners, 2)),
             dma((2,)),
-            dma((6,)),
+            dma((2,)),
+            dma((7,)),
+            dma,
+            dma,
             dma((owners,)),
             dma((2,)),
-            dma((15,)),
+            dma((14,)),
             dma((planes, 2)),
-            dma((2,)),
-            dma((2,)),
+            dma((2, 2)),
+            dma((2, 2)),
             dma((owners,)),
             dma((owners,)),
         ],

time: 88.1 us -> 86.8 us (0.985)
  Pallas kernels: 83.5 us -> 82.1 us
    pallas_call x1, Pallas kernels: 83.5 us -> 82.1 us  [body(): pl.pallas_call(layer_kernel, out_shape=(jax.ShapeDtypeStruct(tokens.shape...]
where the time goes in v6:
time: 86.8 us; the launch traced here: 86.5 us
  Pallas kernels  82.1 us (95%)
  local copies, waits for them, and re-layouts  3.76 us (4%)
    pallas_call x1, Pallas kernels, body(): pl.pallas_call(layer_kernel, out_shape=(jax.ShapeDtypeStruct(tokens.shape...  82.1 us
    unnamed x2, local copies, waits for them, and re-layouts  3.76 us

profile of v6, /device:TPU:1, one launch (start us, length us, event | category | flops | bytes accessed | tf_op | source)
XLA Modules:
  0.0 86.5 jit_solution(17457827933147641212)
XLA Ops:
  0.6 82.1 %layer.1 = (bf16[2,64,2048]{2,1,0:T(8,128)(2,1)}, bf16[2,64,2048]{2,1,0:T(8,128)(2,1)}) custom-call(s32[4,16]{1,0:T(4,128)} %page_table.1, s32[4]{0:T(128)} %prefix_len.1, s32[2]{0:T(128)} %group_of.1, bf16[2,64,2048]{2,1,0:T(8,128)(2,1)} %tokens.1, bf16[128,384]{1,0:T(8,128)(2,1)} %w_ref.1, bf16[64,256]{1,0:T(8,128)(2,1)} %wo_ref.1, ...), custom_call_target="tpu_custom_call" | custom-call | tf_op jit(solution)/shard_map/layer/pallas_call | solution.py:597
  82.8 1.9 %copy.13 = bf16[2,64,2048]{2,1,0:T(8,128)(2,1)} copy(bf16[2,64,2048]{2,1,0:T(8,128)(2,1)} %get-tuple-element.4) | data formatting | bytes 1048576
  84.7 1.9 %copy.14 = bf16[2,64,2048]{2,1,0:T(8,128)(2,1)} copy(bf16[2,64,2048]{2,1,0:T(8,128)(2,1)} %get-tuple-element.5) | data formatting | bytes 1048576
